TPU v7x, 32 devices: a whole 2x2x4 slice. The times are simulated.
32 devices in a mesh: tm: 8 (over z, x), region: 4 (over y, core).
Axes of the slice: x: 2, y: 2, z: 4, core: 2. Of those that a mesh axis runs over, the one named last changes fastest.
Arguments:
- solution: float32 [1024, 4096], P('tm', 'region'), may hold values from -6 to 6
- residual: float32 [1024, 4096], P('tm', 'region'), may hold values from -50 to 50
- direction: float32 [1024, 4096], P('tm', 'region'), may hold values from -50 to 50
- decay: float32 [1024, 4096], P('tm', 'region'), may hold values from 0 to 1, as said below
- spatial: bfloat16 [4096, 4096], P('region'), may hold values from -1 to 2, as said below
- tiles: bfloat16 [8, 4, 8, 128, 512], P('tm', 'region'), may hold values from -0.1875 to 0.1875
- tile_block: int32 [8, 4, 8], P('tm', 'region'), may hold values from 0 to 7
- tile_time: int32 [8, 4, 8], P('tm', 'region'), may hold values from 0 to 383
- tile_cell: int32 [8, 4, 8], P('tm', 'region'), may hold values from 0 to 1
- tile_count: int32 [8, 4], P('tm', 'region'), may hold values from 1 to 8, as said below
- noise_inv: float32 [64, 128], P('tm'), may hold values from 0.25 to 2
Outputs:
- solution_new: float32 [1024, 4096], P('tm', 'region')
- residual_new: float32 [1024, 4096], P('tm', 'region')
- direction_new: float32 [1024, 4096], P('tm', 'region')
Inputs may be any that keep to these rules, and one draw needn't show every extreme that they name: Slots 0 to tile_count - 1 of a window and region hold tiles, the rest are padding; some window and region has 8. `decay`: strictly between 0 and 1. `spatial`: symmetric.
All inputs are finite; a program needn't handle non-finite values.
Results may differ from a plain program's by a relative error of at most 0.0028.
Values may be sent and summed in bfloat16 or wider, within the bound.
No kernel may reach another device: no remote copies, remote signals or barrier semaphores. Data moves between devices by JAX's collectives and lax.ppermute only.
A program may use at most 64 MiB of HBM per device.

v0:
```python
import jax
import jax.numpy as jnp
from jax import lax
from jax.experimental import pallas as pl
from jax.experimental.pallas import tpu as pltpu
from jax.sharding import PartitionSpec as P


FB = 512
BACK = 2
STRIP = 256
SUB = 8
LANES = 128
KERNEL_VMEM = 12 * 2**20


def swapped(block, axis, bit):
    return lax.ppermute(block, axis, [(i, i ^ bit) for i in range(lax.axis_size(axis))])


def shifted(block, axis, distance):
    devices = range(lax.axis_size(axis))
    route = [(i - distance, i) for i in devices if i - distance in devices]
    return lax.ppermute(block, axis, route)


def region_blocks(block):
    blocks, bit = {0: block}, lax.axis_size("region") // 2
    while bit:
        blocks.update({k ^ bit: swapped(b, "region", bit) for k, b in list(blocks.items())})
        bit //= 2
    return blocks


def window_rows(rows):
    bit, pieces = 1, [rows]
    while bit < lax.axis_size("tm"):
        joined = jnp.concatenate(pieces, axis=0) if len(pieces) > 1 else rows
        pieces.append(swapped(joined, "tm", bit))
        bit *= 2
    return pieces


def nt_dot(a, b):
    return lax.dot_general(a, b, (((1,), (1,)), ((), ())), preferred_element_type=jnp.float32)


def strided(start, steps):
    return pl.ds(start, steps // SUB, stride=SUB)


def lanes(k):
    return slice(k * LANES, (k + 1) * LANES)


def on_chip(kernel, scalars, arrays, outs, scratch=(), out_spaces=None, outside=()):
    spaces = out_spaces or [pltpu.VMEM] * len(outs)
    call = pl.pallas_call(
        kernel,
        out_shape=tuple(space(shape, dtype) for space, (shape, dtype) in zip(spaces, outs)),
        in_specs=[pl.BlockSpec(memory_space=pltpu.SMEM)] * len(scalars)
        + [pl.BlockSpec(memory_space=pltpu.VMEM)] * len(arrays)
        + [pl.BlockSpec(memory_space=pl.ANY)] * len(outside),
        out_specs=tuple(pl.BlockSpec(memory_space=pltpu.VMEM) for _ in outs),
        scratch_shapes=list(scratch),
        compiler_params=pltpu.CompilerParams(vmem_limit_bytes=KERNEL_VMEM),
    )
    arrays = [pltpu.with_memory_space_constraint(a, pltpu.VMEM) for a in arrays]
    return call(
        *scalars,
        *arrays,
        *(pltpu.with_memory_space_constraint(a, pltpu.HBM) for a in outside),
    )


def slots_of(place):
    return (place.shape[0] - 1) // 3


def tile_at(place, slot, steps):
    time = place[slot]
    return time // steps, time % steps, place[slots_of(place) + slot] * (FB // LANES)


def product(block, place, region, spatial, strip):
    width = block.shape[1]
    columns = pl.ds(pl.multiple_of((region[0] ^ place) * width, width), width)
    return nt_dot(block[...], spatial[strip * STRIP : (strip + 1) * STRIP, columns])


def first_kernel(region, a_ref, b_ref, spatial, out_ref):
    for strip in range(out_ref.shape[1] // STRIP):
        out_ref[:, strip * STRIP : (strip + 1) * STRIP] = product(
            a_ref, 0, region, spatial, strip
        ) + product(b_ref, 1, region, spatial, strip)


def fetch(region, spatial_hbm, spatial, arrived):
    width = spatial.shape[1] // arrived.shape[0]
    copies = []
    for place in range(arrived.shape[0]):
        columns = pl.ds(pl.multiple_of((region[0] ^ place) * width, width), width)
        copies.append(
            pltpu.make_async_copy(
                spatial_hbm.at[:, columns], spatial.at[:, columns], arrived.at[place]
            )
        )
        copies[-1].start()
    return copies


def fetch_kernel(region, a_ref, b_ref, spatial_hbm, part_ref, spatial, arrived):
    copies = fetch(region, spatial_hbm, spatial, arrived)
    copies[0].wait()
    copies[1].wait()
    first_kernel(region, a_ref, b_ref, spatial, part_ref)
    for copy in copies[2:]:
        copy.wait()


def second_kernel(region, a_ref, spatial, part_ref, out_ref):
    for strip in range(out_ref.shape[1] // STRIP):
        at = slice(strip * STRIP, (strip + 1) * STRIP)
        out_ref[:, at] = part_ref[:, at] + product(a_ref, 2, region, spatial, strip)


def prepare_kernel(
    region,
    a_ref,
    b_ref,
    decay_hbm,
    spatial_hbm,
    part_ref,
    prefix_ref,
    decays_ref,
    gains_ref,
    last_ref,
    spatial,
    arrived,
    decay_arrived,
):
    steps, width = a_ref.shape
    tiles = steps // SUB
    decay_copies = []
    for k in range(width // LANES):
        decay_copies.append(
            pltpu.make_async_copy(
                decay_hbm.at[:, pl.ds(k * LANES, LANES)], decays_ref.at[k], decay_arrived.at[k]
            )
        )
        decay_copies[-1].start()
    copies = fetch(region, spatial_hbm, spatial, arrived)
    for k in range(width // LANES):
        decay_copies[k].wait()
        decay = decays_ref[k]
        gains_ref[k] = jnp.sqrt(1.0 - decay * decay)
        running = [decays_ref[k, strided(0, steps), :]]
        for s in range(1, SUB):
            running.append(running[-1] * decays_ref[k, strided(s, steps), :])
        state = jnp.ones((1, LANES), jnp.float32)
        carried = []
        for b in range(tiles):
            carried.append(state)
            state = state * running[-1][b : b + 1, :]
        last_ref[:, lanes(k)] = state
        carried = jnp.concatenate(carried, axis=0)
        for s in range(SUB):
            prefix_ref[k, strided(s, steps), :] = running[s] * carried
    copies[0].wait()
    copies[1].wait()
    first_kernel(region, a_ref, b_ref, spatial, part_ref)
    for copy in copies[2:]:
        copy.wait()


def filter_kernel(
    region, b_ref, spatial, part_ref, decays, gains, last_ref, local, end_ref
):
    steps, width = b_ref.shape
    tiles = steps // SUB
    end_ref[0:1, :] = last_ref[...]
    for strip in range(width // STRIP):
        mixed = part_ref[:, strip * STRIP : (strip + 1) * STRIP] + product(
            b_ref, 3, region, spatial, strip
        )
        for k in range(strip * STRIP // LANES, (strip + 1) * STRIP // LANES):
            first = k * LANES - strip * STRIP
            local[k] = gains[k] * mixed[:, first : first + LANES]
            state = local[k, strided(0, steps), :]
            factor = decays[k, strided(0, steps), :]
            states, factors = [state], [factor]
            for s in range(1, SUB):
                step_decay = decays[k, strided(s, steps), :]
                state = step_decay * state + local[k, strided(s, steps), :]
                factor = step_decay * factor
                states.append(state)
                factors.append(factor)
            carry = jnp.zeros((1, LANES), jnp.float32)
            entering = []
            for b in range(tiles):
                entering.append(carry)
                carry = factor[b : b + 1, :] * carry + state[b : b + 1, :]
            end_ref[1:2, lanes(k)] = carry
            entering = jnp.concatenate(entering, axis=0)
            for s in range(SUB):
                local[k, strided(s, steps), :] = states[s] + factors[s] * entering


def gather_kernel(own, near, far, local, prefix_ref, own_ref, near_ref, far_ref):
    steps = local.shape[1]
    capacity = own_ref.shape[0] // 2
    for place, rows_ref in ((own, own_ref), (near, near_ref), (far, far_ref)):
        for slot in range(capacity):
            _, step, first = tile_at(place, slot, steps)
            for k in range(FB // LANES):
                at = (first + k, pl.ds(step, 1))
                rows_ref[slot : slot + 1, lanes(k)] = local[*at, :]
                rows_ref[capacity + slot : capacity + slot + 1, lanes(k)] = prefix_ref[*at, :]


def piece_row(pieces, per, distance, row):
    found = pieces[0][row : row + 1, :]
    for k, piece in enumerate(pieces[1:]):
        inside = jnp.clip(distance - 2**k, 0, 2**k - 1)
        at = piece[pl.ds(inside * per + row, 1), :]
        found = jnp.where(distance >= 2**k, at, found)
    return found


def observe_kernel(steps, pieces, here, place, own_ref, near_ref, far_ref, tiles_ref, *rest):
    ends, (seen_ref, factor_ref, entered, picked) = rest[:pieces], rest[pieces:]
    capacity, soundings, cells = tiles_ref.shape
    windows = 2 ** (pieces - 1)
    width = ends[0].shape[1]
    own = here[0]
    entered[...] = jnp.zeros_like(entered)

    def one(window, state):
        for back in range(BACK + 1):

            @pl.when(window == own - back)
            def _():
                entered[BACK - back : BACK - back + 1, :] = state

        return piece_row(ends, 2, window ^ own, 0) * state + piece_row(ends, 2, window ^ own, 1)

    lax.fori_loop(0, windows, one, jnp.zeros((1, width), jnp.float32), unroll=windows <= 8)
    live = place[3 * capacity]
    for slot in range(capacity):
        which, _, first = tile_at(place, slot, steps)
        columns = pl.ds(pl.multiple_of(first * LANES, FB), FB)
        row, later = slice(slot, slot + 1), slice(capacity + slot, capacity + slot + 1)
        offset = jnp.where(
            which == 2, own_ref[row, :], jnp.where(which == 1, near_ref[row, :], far_ref[row, :])
        )
        factor = jnp.where(
            which == 2, own_ref[later, :], jnp.where(which == 1, near_ref[later, :], far_ref[later, :])
        )
        factor_ref[row, :] = factor
        value = offset + factor * entered[pl.ds(which, 1), columns]
        picked[row, :] = jnp.where(slot < live, value, 0.0)
    rows = picked[...].astype(jnp.bfloat16)
    products = nt_dot(rows, tiles_ref[...].reshape(capacity * soundings, cells))
    blocks = lax.broadcasted_iota(jnp.int32, seen_ref.shape, 0)
    seen = jnp.zeros(seen_ref.shape, jnp.float32)
    for slot in range(capacity):
        part = products[slot : slot + 1, slot * soundings : (slot + 1) * soundings]
        seen = seen + jnp.where(blocks == place[2 * capacity + slot], part, 0.0)
    seen_ref[...] = seen


def adjoint_kernel(
    steps, place, seen_ref, other_ref, noise_ref, tiles_ref, factor_ref, rows_ref, sums_ref, weights
):
    capacity, soundings, cells = tiles_ref.shape
    observed = seen_ref[...] + other_ref[...]
    weights[...] = (observed * noise_ref[...]).astype(jnp.bfloat16).astype(jnp.float32)
    slots = lax.broadcasted_iota(jnp.int32, (capacity, soundings), 0)
    live = place[3 * capacity]
    pieces = []
    for slot in range(capacity):
        picked = weights[pl.ds(place[2 * capacity + slot], 1), :]
        pieces.append(jnp.where((slots == slot) & (slot < live), picked, 0.0))
    spread = jnp.concatenate(pieces, axis=1).astype(jnp.bfloat16)
    rows = jnp.dot(
        spread,
        tiles_ref[...].reshape(capacity * soundings, cells),
        preferred_element_type=jnp.float32,
    )
    rows_ref[...] = rows
    handed = rows * factor_ref[...]
    sums_ref[...] = jnp.zeros_like(sums_ref)
    for slot in range(capacity):
        which, _, first = tile_at(place, slot, steps)
        columns = pl.ds(pl.multiple_of(first * LANES, FB), FB)
        at = pl.ds(which, 1)
        sums_ref[at, columns] = sums_ref[at, columns] + handed[slot : slot + 1, :]


def hold_kernel(
    pieces, here, own, near, far, own_ref, near_ref, far_ref, decays, gains, *rest
):
    ends, sums = rest[:pieces], rest[pieces : 2 * pieces]
    pulled_ref, terms = rest[2 * pieces :]
    steps, width = pulled_ref.shape
    tiles = steps // SUB
    capacity = own_ref.shape[0]
    windows = 2 ** (pieces - 1)
    me = here[0]
    per = sums[0].shape[0]

    def one(hop, state):
        window = windows - 1 - hop
        arriving = jnp.zeros((1, width), jnp.float32)
        for ahead in range(BACK + 1):
            reader = jnp.minimum(window + ahead, windows - 1)
            arriving = arriving + jnp.where(
                window + ahead < windows, piece_row(sums, per, reader ^ me, BACK - ahead), 0.0
            )
        passed = piece_row(ends, 2, window ^ me, 0) * state + arriving
        return jnp.where(window > me, passed, state)

    incoming = lax.fori_loop(
        0, windows - 1, one, jnp.zeros((1, width), jnp.float32), unroll=windows <= 8
    )
    terms[...] = jnp.zeros_like(terms)
    for reader, (place, rows) in enumerate(((own, own_ref), (near, near_ref), (far, far_ref))):
        live = place[3 * capacity]
        for slot in range(capacity):
            which, step, first = tile_at(place, slot, steps)
            mine = (which == BACK - reader) & (slot < live)
            step = pl.ds(step, 1)
            for k in range(FB // LANES):
                terms[first + k, step, :] = terms[first + k, step, :] + jnp.where(
                    mine, rows[slot : slot + 1, lanes(k)], 0.0
                )
    for k in range(width // LANES):
        state = terms[k, strided(SUB - 1, steps), :]
        factor = jnp.ones_like(state)
        states, factors = [state], [factor]
        for s in range(SUB - 2, -1, -1):
            step_decay = decays[k, strided(s + 1, steps), :]
            state = terms[k, strided(s, steps), :] + step_decay * state
            factor = step_decay * factor
            states.append(state)
            factors.append(factor)
        first = decays[k, strided(0, steps), :]
        state, factor = first * state, first * factor
        carry = incoming[:, lanes(k)]
        entering = []
        for b in range(tiles - 1, -1, -1):
            entering.insert(0, carry)
            carry = state[b : b + 1, :] + factor[b : b + 1, :] * carry
        entering = jnp.concatenate(entering, axis=0)
        for s in range(SUB):
            terms[k, strided(SUB - 1 - s, steps), :] = states[s] + factors[s] * entering
        pulled_ref[:, lanes(k)] = (gains[k] * terms[k]).astype(jnp.bfloat16)


def image_kernel(
    region, b_ref, spatial, part_ref, direction_ref, residual_ref, image_ref, sums_ref
):
    _, width = b_ref.shape
    totals = [jnp.zeros((1, STRIP), jnp.float32) for _ in range(4)]
    for strip in range(width // STRIP):
        at = slice(strip * STRIP, (strip + 1) * STRIP)
        direction, residual = direction_ref[:, at], residual_ref[:, at]
        image = direction + (part_ref[:, at] + product(b_ref, 3, region, spatial, strip))
        image_ref[:, at] = image
        terms = (residual * residual, direction * image, residual * image, image * image)
        totals = [t + jnp.sum(term, axis=0, keepdims=True) for t, term in zip(totals, terms)]
    sums_ref[...] = jnp.zeros_like(sums_ref)
    for k, total in enumerate(totals):
        sums_ref[k : k + 1, :] = jnp.broadcast_to(
            jnp.sum(total, axis=1, keepdims=True), (1, LANES)
        )


def update_kernel(
    totals_ref, solution_ref, residual_ref, direction_ref, image_ref, solution_new, residual_new, direction_new
):
    norm_old, curvature, cross_sum, image_sq = (totals_ref[k : k + 1, :] for k in range(4))
    step_len = norm_old / curvature
    norm_new = norm_old - 2.0 * step_len * cross_sum + step_len * step_len * image_sq
    ratio = norm_new / norm_old
    for k in range(direction_ref.shape[1] // LANES):
        direction = direction_ref[:, lanes(k)]
        residual = residual_ref[:, lanes(k)] - step_len * image_ref[:, lanes(k)]
        solution_new[:, lanes(k)] = solution_ref[:, lanes(k)] + step_len * direction
        residual_new[:, lanes(k)] = residual
        direction_new[:, lanes(k)] = residual + ratio * direction


def body(
    solution,
    residual,
    direction,
    decay,
    spatial,
    tiles,
    tile_block,
    tile_time,
    tile_cell,
    tile_count,
    noise_inv,
):
    steps, width = direction.shape
    footprint = tiles[0, 0]
    capacity, soundings, cells = footprint.shape
    block_count = noise_inv.shape[0]
    here = lax.axis_index("tm").astype(jnp.int32).reshape(1)
    region = lax.axis_index("region").astype(jnp.int32).reshape(1)
    f32 = jnp.float32
    columns = pltpu.VMEM((width // LANES, steps, LANES), f32)
    regions = spatial.shape[1] // width

    place = jnp.concatenate([tile_time[0, 0], tile_cell[0, 0], tile_block[0, 0], tile_count[0]])
    half = direction.astype(jnp.bfloat16)
    blocks = region_blocks(half)
    part, prefix, decays, gains, last, kept = on_chip(
        prepare_kernel,
        [region],
        [blocks[0], blocks[1]],
        [((steps, width), f32)]
        + [(columns.shape, f32)] * 3
        + [((1, width), f32), (spatial.shape, spatial.dtype)],
        [pltpu.SemaphoreType.DMA((regions,)), pltpu.SemaphoreType.DMA((width // LANES,))],
        outside=[decay, spatial],
    )
    (part,) = on_chip(second_kernel, [region], [blocks[2], kept, part], [((steps, width), f32)])
    places = [place, shifted(place, "tm", -1), shifted(place, "tm", -2)]
    local, end = on_chip(
        filter_kernel,
        [region],
        [blocks[3], kept, part, decays, gains, last],
        [(columns.shape, f32), ((2, width), f32)],
    )
    own_rows, near_rows, far_rows = on_chip(
        gather_kernel, places, [local, prefix], [((2 * capacity, cells), f32)] * (BACK + 1)
    )
    near_rows = shifted(near_rows, "tm", 1)
    far_rows = shifted(far_rows, "tm", 2)
    ends = window_rows(end)
    seen, factors = on_chip(
        lambda *refs: observe_kernel(steps, len(ends), *refs),
        [here, place],
        [own_rows, near_rows, far_rows, footprint] + ends,
        [((block_count, soundings), f32), ((capacity, cells), f32)],
        [pltpu.VMEM((SUB, width), f32), pltpu.VMEM((capacity, cells), f32)],
    )
    bit = 1
    while bit < lax.axis_size("region") // 2:
        seen = seen + swapped(seen, "region", bit)
        bit *= 2
    rows, sums = on_chip(
        lambda *refs: adjoint_kernel(steps, *refs),
        [place],
        [seen, swapped(seen, "region", bit), noise_inv, footprint, factors],
        [((capacity, cells), f32), ((BACK + 2, width), f32)],
        [pltpu.VMEM(noise_inv.shape, f32)],
    )
    near_rows = shifted(rows, "tm", -1)
    far_rows = shifted(rows, "tm", -2)
    (pulled,) = on_chip(
        lambda *refs: hold_kernel(len(ends), *refs),
        [here] + places,
        [rows, near_rows, far_rows, decays, gains] + ends + window_rows(sums),
        [((steps, width), jnp.bfloat16)],
        [columns],
    )
    blocks = region_blocks(pulled)
    part, kept = on_chip(
        fetch_kernel,
        [region],
        [blocks[0], blocks[1]],
        [((steps, width), f32), (spatial.shape, spatial.dtype)],
        [pltpu.SemaphoreType.DMA((regions,))],
        outside=[spatial],
    )
    (part,) = on_chip(second_kernel, [region], [blocks[2], kept, part], [((steps, width), f32)])
    image, totals = on_chip(
        image_kernel,
        [region],
        [blocks[3], kept, part, direction, residual],
        [((steps, width), f32), ((SUB, LANES), f32)],
    )
    for axis in ("region", "tm"):
        bit = 1
        while bit < lax.axis_size(axis):
            totals = totals + swapped(totals, axis, bit)
            bit *= 2
    return on_chip(
        update_kernel,
        [],
        [totals, solution, residual, direction, image],
        [((steps, width), f32)] * 3,
        out_spaces=[jax.ShapeDtypeStruct] * 3,
    )


def solution(mesh):
    return jax.shard_map(
        body,
        mesh=mesh,
        in_specs=(
            P("tm", "region"),
            P("tm", "region"),
            P("tm", "region"),
            P("tm", "region"),
            P("region", None),
            P("tm", "region", None, None, None),
            P("tm", "region", None),
            P("tm", "region", None),
            P("tm", "region", None),
            P("tm", "region"),
            P("tm", None),
        ),
        out_specs=(P("tm", "region"), P("tm", "region"), P("tm", "region")),
        check_vma=False,
    )
```

profile of v0, /device:TPU:0, one launch (start us, length us, event | category | flops | bytes accessed | tf_op | source)
XLA Modules:
  0.0 98.5 jit_solution(15689659684476402174)
XLA Ops:
  0.6 1.1 %convert_element_type.3.a_ref = bf16[128,1024]{1,0:T(8,128)(2,1)S(1)} convert(f32[128,1024]{1,0:T(8,128)} %direction_ref.3) | non-fusion elementwise | flops 131072 | bytes 786432 | tf_op jit(solution)/shard_map/convert_element_type | solution.py:418
  1.7 3.1 %collective-permute-start.2 = (bf16[128,1024]{1,0:T(8,128)(2,1)S(1)}, bf16[128,1024]{1,0:T(8,128)(2,1)S(1)}, u32[]{:S(2)}, u32[]{:S(2)}) collective-permute-start(bf16[128,1024]{1,0:T(8,128)(2,1)S(1)} %convert_element_type.3.a_ref), channel_id=1, source_target_pairs={{0,2},{1,3},{2,0},{3,1},{4,6},{5,7},{6,4},{7,5},{8,10},{9,11},{10,... | collective-permute-start | bytes 786440 | tf_op jit(solution)/shard_map/ppermute | solution.py:18
  4.8 0.0 collective-permute-start.4
  4.8 6.3 %collective-permute-done.2.a_ref = bf16[128,1024]{1,0:T(8,128)(2,1)S(1)} collective-permute-done((bf16[128,1024]{1,0:T(8,128)(2,1)S(1)}, bf16[128,1024]{1,0:T(8,128)(2,1)S(1)}, u32[]{:S(2)}, u32[]{:S(2)}) %collective-permute-start.2) | collective-permute-done | bytes 262176 | tf_op jit(solution)/shard_map/ppermute | solution.py:18
  11.1 0.0 collective-permute-start.3
  11.1 4.6 %shard_map.130 = (f32[128,1024]{1,0:T(8,128)S(1)}, f32[8,128,128]{2,1,0:T(8,128)S(1)}, f32[8,128,128]{2,1,0:T(8,128)S(1)}, f32[8,128,128]{2,1,0:T(8,128)S(1)}, f...) custom-call(s32[1]{0:T(128)} %bitcast.region, bf16[128,1024]{1,0:T(8,128)(2,1)S(1)} %convert_element_type.3.a_ref, ...), custom_call_target="tpu_custom_call" | custom-call | tf_op jit(solution)/shard_map/pallas_call | solution.py:69
  15.7 0.0 copy-start.5
  15.7 0.0 copy-start.6
  15.7 0.0 copy-start.7
  15.7 0.0 copy-start.1
  15.8 0.8 shard_map.131.part_ref
  16.6 0.0 copy-start.4
  16.6 0.0 collective-permute-done.3.b_ref
  16.6 1.1 %shard_map.132 = (f32[8,128,128]{2,1,0:T(8,128)S(1)}, f32[2,1024]{1,0:T(2,128)S(1)}) custom-call(s32[1]{0:T(128)} %bitcast.region, bf16[128,1024]{1,0:T(8,128)(2,1)S(1)} %collective-permute-done.3.b_ref, bf16[1024,4096]{1,0:T(8,128)(2,1)S(1)} %get-tuple-element.22.spatial, f32[128,1024]{1,0:T(8,128)S(1)} %shard_map.131.part_ref, ...), custom_call_target="tpu_custom_call" | custom-call | tf_op jit(solution)/shard_map/pallas_call | solution.py:69
  17.7 1.8 %collective-permute-start.7 = (f32[2,1024]{1,0:T(2,128)S(1)}, f32[2,1024]{1,0:T(2,128)S(1)}, u32[]{:S(2)}, u32[]{:S(2)}) collective-permute-start(f32[2,1024]{1,0:T(2,128)S(1)} %get-tuple-element.32.refs_6_.refs_9_), channel_id=1, source_target_pairs={{0,4},{4,0},{8,12},{12,8},{16,20},{20,16},{24,28},{28,24},{1,5},{5... | collective-permute-start | bytes 24584 | tf_op jit(solution)/shard_map/ppermute | solution.py:18
  20.1 1.3 %collective-permute-done.7.refs_7_.refs_10_ = f32[2,1024]{1,0:T(2,128)S(1)} collective-permute-done((f32[2,1024]{1,0:T(2,128)S(1)}, f32[2,1024]{1,0:T(2,128)S(1)}, u32[]{:S(2)}, u32[]{:S(2)}) %collective-permute-start.7) | collective-permute-done | bytes 8224 | tf_op jit(solution)/shard_map/ppermute | solution.py:18
  21.4 1.9 %collective-permute-start.8 = (f32[4,1024]{1,0:T(4,128)S(1)}, f32[4,1024]{1,0:T(4,128)S(1)}, u32[]{:S(2)}, u32[]{:S(2)}) collective-permute-start(f32[4,1024]{1,0:T(4,128)S(1)} %pad_maximum_fusion.3), channel_id=1, source_target_pairs={{0,8},{4,12},{8,0},{12,4},{16,24},{20,28},{24,16},{28,20},{1,9},{5... | collective-permute-start | bytes 49160 | tf_op jit(solution)/shard_map/ppermute | solution.py:18
  23.3 0.1 pad_add_fusion.own.refs_1_.refs_0_
  23.4 1.3 %collective-permute-start = (s32[25]{0:T(128)S(1)}, s32[25]{0:T(128)S(1)}, u32[]{:S(2)}, u32[]{:S(2)}) collective-permute-start(s32[25]{0:T(128)S(1)} %pad_add_fusion.own.refs_1_.refs_0_), channel_id=1, source_target_pairs={{4,0},{8,4},{12,8},{16,12},{20,16},{24,20},{28,24},{5,1},{9,5},{13... | collective-permute-start | bytes 308 | tf_op jit(solution)/shard_map/ppermute | solution.py:24
  24.7 1.3 %collective-permute-start.1 = (s32[25]{0:T(128)S(1)}, s32[25]{0:T(128)S(1)}, u32[]{:S(2)}, u32[]{:S(2)}) collective-permute-start(s32[25]{0:T(128)S(1)} %pad_add_fusion.own.refs_1_.refs_0_), channel_id=1, source_target_pairs={{8,0},{12,4},{16,8},{20,12},{24,16},{28,20},{9,1},{13,5},{17,9},{2... | collective-permute-start | bytes 308 | tf_op jit(solution)/shard_map/ppermute | solution.py:24
  26.0 2.9 %collective-permute-done.near.refs_2_ = s32[25]{0:T(128)S(1)} collective-permute-done((s32[25]{0:T(128)S(1)}, s32[25]{0:T(128)S(1)}, u32[]{:S(2)}, u32[]{:S(2)}) %collective-permute-start) | collective-permute-done | bytes 132 | tf_op jit(solution)/shard_map/ppermute | solution.py:24
  28.8 2.9 %collective-permute-done.1.far.refs_3_ = s32[25]{0:T(128)S(1)} collective-permute-done((s32[25]{0:T(128)S(1)}, s32[25]{0:T(128)S(1)}, u32[]{:S(2)}, u32[]{:S(2)}) %collective-permute-start.1) | collective-permute-done | bytes 132 | tf_op jit(solution)/shard_map/ppermute | solution.py:24
  31.7 0.7 shard_map.133
  32.4 3.0 %collective-permute-start.5 = (f32[16,512]{1,0:T(8,128)S(1)}, f32[16,512]{1,0:T(8,128)S(1)}, u32[]{:S(2)}, u32[]{:S(2)}) collective-permute-start(f32[16,512]{1,0:T(8,128)S(1)} %get-tuple-element.30), channel_id=1, source_target_pairs={{0,4},{4,8},{8,12},{12,16},{16,20},{20,24},{24,28},{1,5},{5,9},{9,... | collective-permute-start | bytes 98312 | tf_op jit(solution)/shard_map/ppermute | solution.py:24
  35.4 3.0 %collective-permute-start.6 = (f32[16,512]{1,0:T(8,128)S(1)}, f32[16,512]{1,0:T(8,128)S(1)}, u32[]{:S(2)}, u32[]{:S(2)}) collective-permute-start(f32[16,512]{1,0:T(8,128)S(1)} %get-tuple-element.31), channel_id=1, source_target_pairs={{0,8},{4,12},{8,16},{12,20},{16,24},{20,28},{1,9},{5,13},{9,17},{1... | collective-permute-start | bytes 98312 | tf_op jit(solution)/shard_map/ppermute | solution.py:24
  38.4 0.0 collective-permute-done.8.refs_8_.refs_11_
  38.5 1.5 %collective-permute-start.9 = (f32[8,1024]{1,0:T(8,128)S(1)}, f32[8,1024]{1,0:T(8,128)S(1)}, u32[]{:S(2)}, u32[]{:S(2)}) collective-permute-start(f32[8,1024]{1,0:T(8,128)S(1)} %pad_maximum_fusion.1), channel_id=1, source_target_pairs={{0,16},{4,20},{8,24},{12,28},{16,0},{20,4},{24,8},{28,12},{1,17},{... | collective-permute-start | bytes 98312 | tf_op jit(solution)/shard_map/ppermute | solution.py:18
  40.0 0.0 collective-permute-done.6.refs_4_
  40.0 3.3 %collective-permute-done.9.refs_9_.refs_12_ = f32[8,1024]{1,0:T(8,128)S(1)} collective-permute-done((f32[8,1024]{1,0:T(8,128)S(1)}, f32[8,1024]{1,0:T(8,128)S(1)}, u32[]{:S(2)}, u32[]{:S(2)}) %collective-permute-start.9) | collective-permute-done | bytes 32800 | tf_op jit(solution)/shard_map/ppermute | solution.py:18
  43.3 1.1 %shard_map.134 = (f32[8,128]{1,0:T(8,128)S(1)}, f32[8,512]{1,0:T(8,128)S(1)}) custom-call(s32[1]{0:T(128)} %bitcast.1.refs_0_, s32[25]{0:T(128)S(1)} %pad_add_fusion.own.refs_1_.refs_0_, f32[16,512]{1,0:T(8,128)S(1)} %get-tuple-element.29.refs_2_, f32[16,512]{1,0:T(8,128)S(1)} %collective-permute-done.5.refs_3_, ...), custom_call_target="tpu_custom_call" | custom-call | tf_op jit(solution)/shard_map/pallas_call | solution.py:69
  44.5 0.0 collective-permute-start.10
  44.5 1.2 %collective-permute-done.10 = f32[8,128]{1,0:T(8,128)S(1)} collective-permute-done((f32[8,128]{1,0:T(8,128)S(1)}, f32[8,128]{1,0:T(8,128)S(1)}, u32[]{:S(2)}, u32[]{:S(2)}) %collective-permute-start.10) | collective-permute-done | bytes 4128 | tf_op jit(solution)/shard_map/ppermute | solution.py:18
  45.7 1.5 %collective-permute-start.11 = (f32[8,128]{1,0:T(8,128)S(1)}, f32[8,128]{1,0:T(8,128)S(1)}, u32[]{:S(2)}, u32[]{:S(2)}) collective-permute-start(f32[8,128]{1,0:T(8,128)S(1)} %add.18.refs_1_), channel_id=1, source_target_pairs={{0,2},{1,3},{2,0},{3,1},{4,6},{5,7},{6,4},{7,5},{8,10},{9,11},{10,... | collective-permute-start | bytes 12296 | tf_op jit(solution)/shard_map/ppermute | solution.py:18
  47.2 2.1 %collective-permute-done.11.refs_2_ = f32[8,128]{1,0:T(8,128)S(1)} collective-permute-done((f32[8,128]{1,0:T(8,128)S(1)}, f32[8,128]{1,0:T(8,128)S(1)}, u32[]{:S(2)}, u32[]{:S(2)}) %collective-permute-start.11) | collective-permute-done | bytes 4128 | tf_op jit(solution)/shard_map/ppermute | solution.py:18
  49.3 0.8 shard_map.135
  50.1 1.9 %collective-permute-start.14 = (f32[4,1024]{1,0:T(4,128)S(1)}, f32[4,1024]{1,0:T(4,128)S(1)}, u32[]{:S(2)}, u32[]{:S(2)}) collective-permute-start(f32[4,1024]{1,0:T(4,128)S(1)} %get-tuple-element.36.refs_13_), channel_id=1, source_target_pairs={{0,4},{4,0},{8,12},{12,8},{16,20},{20,16},{24,28},{28,24},{1,5},{5... | collective-permute-start | bytes 49160 | tf_op jit(solution)/shard_map/ppermute | solution.py:18
  52.0 1.9 %collective-permute-done.14.refs_14_ = f32[4,1024]{1,0:T(4,128)S(1)} collective-permute-done((f32[4,1024]{1,0:T(4,128)S(1)}, f32[4,1024]{1,0:T(4,128)S(1)}, u32[]{:S(2)}, u32[]{:S(2)}) %collective-permute-start.14) | collective-permute-done | bytes 16416 | tf_op jit(solution)/shard_map/ppermute | solution.py:18
  53.9 2.1 %collective-permute-start.15 = (f32[8,1024]{1,0:T(8,128)S(1)}, f32[8,1024]{1,0:T(8,128)S(1)}, u32[]{:S(2)}, u32[]{:S(2)}) collective-permute-start(f32[8,1024]{1,0:T(8,128)S(1)} %pad_maximum_fusion.2), channel_id=1, source_target_pairs={{0,8},{4,12},{8,0},{12,4},{16,24},{20,28},{24,16},{28,20},{1,9},{5... | collective-permute-start | bytes 98312 | tf_op jit(solution)/shard_map/ppermute | solution.py:18
  56.0 1.9 %collective-permute-done.15.refs_15_ = f32[8,1024]{1,0:T(8,128)S(1)} collective-permute-done((f32[8,1024]{1,0:T(8,128)S(1)}, f32[8,1024]{1,0:T(8,128)S(1)}, u32[]{:S(2)}, u32[]{:S(2)}) %collective-permute-start.15) | collective-permute-done | bytes 32800 | tf_op jit(solution)/shard_map/ppermute | solution.py:18
  57.9 1.5 %collective-permute-start.16 = (f32[16,1024]{1,0:T(8,128)S(1)}, f32[16,1024]{1,0:T(8,128)S(1)}, u32[]{:S(2)}, u32[]{:S(2)}) collective-permute-start(f32[16,1024]{1,0:T(8,128)S(1)} %pad_maximum_fusion), channel_id=1, source_target_pairs={{0,16},{4,20},{8,24},{12,28},{16,0},{20,4},{24,8},{28,12},{1,17},{... | collective-permute-start | bytes 196616 | tf_op jit(solution)/shard_map/ppermute | solution.py:18
  59.4 1.3 %collective-permute-start.12 = (f32[8,512]{1,0:T(8,128)S(1)}, f32[8,512]{1,0:T(8,128)S(1)}, u32[]{:S(2)}, u32[]{:S(2)}) collective-permute-start(f32[8,512]{1,0:T(8,128)S(1)} %get-tuple-element.35.refs_4_), channel_id=1, source_target_pairs={{4,0},{8,4},{12,8},{16,12},{20,16},{24,20},{28,24},{5,1},{9,5},{13... | collective-permute-start | bytes 49160 | tf_op jit(solution)/shard_map/ppermute | solution.py:24
  60.7 1.3 %collective-permute-start.13 = (f32[8,512]{1,0:T(8,128)S(1)}, f32[8,512]{1,0:T(8,128)S(1)}, u32[]{:S(2)}, u32[]{:S(2)}) collective-permute-start(f32[8,512]{1,0:T(8,128)S(1)} %get-tuple-element.35.refs_4_), channel_id=1, source_target_pairs={{8,0},{12,4},{16,8},{20,12},{24,16},{28,20},{9,1},{13,5},{17,9},{2... | collective-permute-start | bytes 49160 | tf_op jit(solution)/shard_map/ppermute | solution.py:24
  62.0 3.0 %collective-permute-done.12.refs_5_ = f32[8,512]{1,0:T(8,128)S(1)} collective-permute-done((f32[8,512]{1,0:T(8,128)S(1)}, f32[8,512]{1,0:T(8,128)S(1)}, u32[]{:S(2)}, u32[]{:S(2)}) %collective-permute-start.12) | collective-permute-done | bytes 16416 | tf_op jit(solution)/shard_map/ppermute | solution.py:24
  65.1 1.9 %collective-permute-done.13.refs_6_ = f32[8,512]{1,0:T(8,128)S(1)} collective-permute-done((f32[8,512]{1,0:T(8,128)S(1)}, f32[8,512]{1,0:T(8,128)S(1)}, u32[]{:S(2)}, u32[]{:S(2)}) %collective-permute-start.13) | collective-permute-done | bytes 16416 | tf_op jit(solution)/shard_map/ppermute | solution.py:24
  67.0 1.3 %shard_map.136.a_ref = bf16[128,1024]{1,0:T(8,128)(2,1)S(1)} custom-call(s32[1]{0:T(128)} %bitcast.1.refs_0_, s32[25]{0:T(128)S(1)} %pad_add_fusion.own.refs_1_.refs_0_, s32[25]{0:T(128)S(1)} %collective-permute-done.near.refs_2_, s32[25]{0:T(128)S(1)} %collective-permute-done.1.far.refs_3_, f32[8,512]{1,0:T(8,128)S(1)} %get-tuple-element.35.refs_4_, ...), custom_call_target="tpu_custom_call" | custom-call | tf_op jit(solution)/shard_map/pallas_call | solution.py:69
  68.3 0.0 copy-start
  68.3 0.0 copy-start.2
  68.3 1.6 %collective-permute-start.17 = (bf16[128,1024]{1,0:T(8,128)(2,1)S(1)}, bf16[128,1024]{1,0:T(8,128)(2,1)S(1)}, u32[]{:S(2)}, u32[]{:S(2)}) collective-permute-start(bf16[128,1024]{1,0:T(8,128)(2,1)S(1)} %shard_map.136.a_ref), channel_id=1, source_target_pairs={{0,2},{1,3},{2,0},{3,1},{4,6},{5,7},{6,4},{7,5},{8,10},{9,11},{10,... | collective-permute-start | bytes 786440 | tf_op jit(solution)/shard_map/ppermute | solution.py:18
  69.9 4.8 %collective-permute-done.17.a_ref = bf16[128,1024]{1,0:T(8,128)(2,1)S(1)} collective-permute-done((bf16[128,1024]{1,0:T(8,128)(2,1)S(1)}, bf16[128,1024]{1,0:T(8,128)(2,1)S(1)}, u32[]{:S(2)}, u32[]{:S(2)}) %collective-permute-start.17) | collective-permute-done | bytes 262176 | tf_op jit(solution)/shard_map/ppermute | solution.py:18
  74.7 3.8 %shard_map.137 = (f32[128,1024]{1,0:T(8,128)S(1)}, bf16[1024,4096]{1,0:T(8,128)(2,1)S(1)}) custom-call(s32[1]{0:T(128)} %bitcast.region, bf16[128,1024]{1,0:T(8,128)(2,1)S(1)} %shard_map.136.a_ref, bf16[128,1024]{1,0:T(8,128)(2,1)S(1)} %collective-permute-done.19.b_ref, bf16[1024,4096]{1,0:T(8,128)(2,1)} %spatial_hbm.3), custom_call_target="tpu_custom_call" | custom-call | tf_op jit(solution)/shard_map/pallas_call | solution.py:69
  78.5 0.0 copy-start.3
  78.6 0.8 shard_map.138.part_ref
  79.4 1.0 %shard_map.139 = (f32[128,1024]{1,0:T(8,128)S(1)}, f32[8,128]{1,0:T(8,128)S(1)}) custom-call(s32[1]{0:T(128)} %bitcast.region, bf16[128,1024]{1,0:T(8,128)(2,1)S(1)} %collective-permute-done.18.b_ref, bf16[1024,4096]{1,0:T(8,128)(2,1)S(1)} %get-tuple-element.37.spatial, f32[128,1024]{1,0:T(8,128)S(1)} %shard_map.138.part_ref, f32[128,1024]{1,0:T(8,128)S(1)} %copy-done, ...), custom_call_target="tpu_custom_call" | custom-call | tf_op jit(solution)/shard_map/pallas_call | solution.py:69
  80.4 0.5 collective-permute-start.20
  80.9 0.8 collective-permute-done.20
  81.8 1.5 %collective-permute-start.21 = (f32[8,128]{1,0:T(8,128)S(1)}, f32[8,128]{1,0:T(8,128)S(1)}, u32[]{:S(2)}, u32[]{:S(2)}) collective-permute-start(f32[8,128]{1,0:T(8,128)S(1)} %add.19), channel_id=1, source_target_pairs={{0,2},{1,3},{2,0},{3,1},{4,6},{5,7},{6,4},{7,5},{8,10},{9,11},{10,... | collective-permute-start | bytes 12296 | tf_op jit(solution)/shard_map/ppermute | solution.py:18
  83.3 2.1 %collective-permute-done.21 = f32[8,128]{1,0:T(8,128)S(1)} collective-permute-done((f32[8,128]{1,0:T(8,128)S(1)}, f32[8,128]{1,0:T(8,128)S(1)}, u32[]{:S(2)}, u32[]{:S(2)}) %collective-permute-start.21) | collective-permute-done | bytes 4128 | tf_op jit(solution)/shard_map/ppermute | solution.py:18
  85.4 2.1 %collective-permute-start.22 = (f32[8,128]{1,0:T(8,128)S(1)}, f32[8,128]{1,0:T(8,128)S(1)}, u32[]{:S(2)}, u32[]{:S(2)}) collective-permute-start(f32[8,128]{1,0:T(8,128)S(1)} %add.20), channel_id=1, source_target_pairs={{0,4},{4,0},{8,12},{12,8},{16,20},{20,16},{24,28},{28,24},{1,5},{5... | collective-permute-start | bytes 12296 | tf_op jit(solution)/shard_map/ppermute | solution.py:18
  87.4 1.6 %collective-permute-done.22 = f32[8,128]{1,0:T(8,128)S(1)} collective-permute-done((f32[8,128]{1,0:T(8,128)S(1)}, f32[8,128]{1,0:T(8,128)S(1)}, u32[]{:S(2)}, u32[]{:S(2)}) %collective-permute-start.22) | collective-permute-done | bytes 4128 | tf_op jit(solution)/shard_map/ppermute | solution.py:18
  89.0 2.0 %collective-permute-start.23 = (f32[8,128]{1,0:T(8,128)S(1)}, f32[8,128]{1,0:T(8,128)S(1)}, u32[]{:S(2)}, u32[]{:S(2)}) collective-permute-start(f32[8,128]{1,0:T(8,128)S(1)} %add.21), channel_id=1, source_target_pairs={{0,8},{4,12},{8,0},{12,4},{16,24},{20,28},{24,16},{28,20},{1,9},{5... | collective-permute-start | bytes 12296 | tf_op jit(solution)/shard_map/ppermute | solution.py:18
  91.0 1.6 %collective-permute-done.23 = f32[8,128]{1,0:T(8,128)S(1)} collective-permute-done((f32[8,128]{1,0:T(8,128)S(1)}, f32[8,128]{1,0:T(8,128)S(1)}, u32[]{:S(2)}, u32[]{:S(2)}) %collective-permute-start.23) | collective-permute-done | bytes 4128 | tf_op jit(solution)/shard_map/ppermute | solution.py:18
  92.6 2.1 %collective-permute-start.24 = (f32[8,128]{1,0:T(8,128)S(1)}, f32[8,128]{1,0:T(8,128)S(1)}, u32[]{:S(2)}, u32[]{:S(2)}) collective-permute-start(f32[8,128]{1,0:T(8,128)S(1)} %add.22), channel_id=1, source_target_pairs={{0,16},{4,20},{8,24},{12,28},{16,0},{20,4},{24,8},{28,12},{1,17},{... | collective-permute-start | bytes 12296 | tf_op jit(solution)/shard_map/ppermute | solution.py:18
  94.7 2.4 %collective-permute-done.24 = f32[8,128]{1,0:T(8,128)S(1)} collective-permute-done((f32[8,128]{1,0:T(8,128)S(1)}, f32[8,128]{1,0:T(8,128)S(1)}, u32[]{:S(2)}, u32[]{:S(2)}) %collective-permute-start.24) | collective-permute-done | bytes 4128 | tf_op jit(solution)/shard_map/ppermute | solution.py:18
  97.2 1.3 %shard_map.140 = (f32[128,1024]{1,0:T(8,128)}, f32[128,1024]{1,0:T(8,128)}, f32[128,1024]{1,0:T(8,128)}) custom-call(f32[8,128]{1,0:T(8,128)S(1)} %add.23.totals_ref, f32[128,1024]{1,0:T(8,128)S(1)} %copy-done.3, f32[128,1024]{1,0:T(8,128)S(1)} %copy-done.2, f32[128,1024]{1,0:T(8,128)S(1)} %copy-done, f32[128,1024]{1,0:T(8,128)S(1)} %get-tuple-element.40.image_ref), custom_call_target="tpu_custom_call" | custom-call | tf_op jit(solution)/shard_map/pallas_call | solution.py:69
  (25 shorter events, 0.1 us)
Async XLA Ops:
  1.7 9.4 %collective-permute-start.2 = (bf16[128,1024]{1,0:T(8,128)(2,1)S(1)}, bf16[128,1024]{1,0:T(8,128)(2,1)S(1)}, u32[]{:S(2)}, u32[]{:S(2)}) collective-permute-start(bf16[128,1024]{1,0:T(8,128)(2,1)S(1)} %convert_element_type.3.a_ref), channel_id=1, source_target_pairs={{0,2},{1,3},{2,0},{3,1},{4,6},{5,7},{6,4},{7,5},{8,10},{9,11},{10,... | collective-permute-start | bytes 786440 | tf_op jit(solution)/shard_map/ppermute | solution.py:18
  4.8 6.3 %collective-permute-start.4 = (bf16[128,1024]{1,0:T(8,128)(2,1)S(1)}, bf16[128,1024]{1,0:T(8,128)(2,1)S(1)}, u32[]{:S(2)}, u32[]{:S(2)}) collective-permute-start(bf16[128,1024]{1,0:T(8,128)(2,1)S(1)} %convert_element_type.3.a_ref), channel_id=1, source_target_pairs={{0,1},{1,0},{2,3},{3,2},{4,5},{5,4},{6,7},{7,6},{8,9},{9,8},{10,11... | collective-permute-start | bytes 786440 | tf_op jit(solution)/shard_map/ppermute | solution.py:18
  11.1 5.5 %collective-permute-start.3 = (bf16[128,1024]{1,0:T(8,128)(2,1)S(1)}, bf16[128,1024]{1,0:T(8,128)(2,1)S(1)}, u32[]{:S(2)}, u32[]{:S(2)}) collective-permute-start(bf16[128,1024]{1,0:T(8,128)(2,1)S(1)} %collective-permute-done.2.a_ref), channel_id=1, source_target_pairs={{0,1},{1,0},{2,3},{3,2},{4,5},{5,4},{6,7},{7,6},{8,9},{9,8},{10,11... | collective-permute-start | bytes 786440 | tf_op jit(solution)/shard_map/ppermute | solution.py:18
  15.7 7.6 %copy-start.5 = (s32[1,1,8]{2,1,0:T(1,128)S(1)}, s32[1,1,8]{2,1,0:T(1,128)}, u32[]{:S(2)}) copy-start(s32[1,1,8]{2,1,0:T(1,128)} %param.17) | copy-start | bytes 100
  15.7 7.6 %copy-start.6 = (s32[1,1,8]{2,1,0:T(1,128)S(1)}, s32[1,1,8]{2,1,0:T(1,128)}, u32[]{:S(2)}) copy-start(s32[1,1,8]{2,1,0:T(1,128)} %param.19) | copy-start | bytes 100
  15.7 7.6 %copy-start.7 = (s32[1,1,8]{2,1,0:T(1,128)S(1)}, s32[1,1,8]{2,1,0:T(1,128)}, u32[]{:S(2)}) copy-start(s32[1,1,8]{2,1,0:T(1,128)} %param.18) | copy-start | bytes 100
  15.7 27.6 %copy-start.1 = (bf16[1,1,8,128,512]{4,3,2,1,0:T(8,128)(2,1)S(1)}, bf16[1,1,8,128,512]{4,3,2,1,0:T(8,128)(2,1)}, u32[]{:S(2)}) copy-start(bf16[1,1,8,128,512]{4,3,2,1,0:T(8,128)(2,1)} %param.16) | copy-start | bytes 3145732
  16.6 32.7 %copy-start.4 = (f32[8,128]{1,0:T(8,128)S(1)}, f32[8,128]{1,0:T(8,128)}, u32[]{:S(2)}) copy-start(f32[8,128]{1,0:T(8,128)} %refs_3_.1) | copy-start | bytes 12292
  17.7 3.7 %collective-permute-start.7 = (f32[2,1024]{1,0:T(2,128)S(1)}, f32[2,1024]{1,0:T(2,128)S(1)}, u32[]{:S(2)}, u32[]{:S(2)}) collective-permute-start(f32[2,1024]{1,0:T(2,128)S(1)} %get-tuple-element.32.refs_6_.refs_9_), channel_id=1, source_target_pairs={{0,4},{4,0},{8,12},{12,8},{16,20},{20,16},{24,28},{28,24},{1,5},{5... | collective-permute-start | bytes 24584 | tf_op jit(solution)/shard_map/ppermute | solution.py:18
  21.4 17.0 %collective-permute-start.8 = (f32[4,1024]{1,0:T(4,128)S(1)}, f32[4,1024]{1,0:T(4,128)S(1)}, u32[]{:S(2)}, u32[]{:S(2)}) collective-permute-start(f32[4,1024]{1,0:T(4,128)S(1)} %pad_maximum_fusion.3), channel_id=1, source_target_pairs={{0,8},{4,12},{8,0},{12,4},{16,24},{20,28},{24,16},{28,20},{1,9},{5... | collective-permute-start | bytes 49160 | tf_op jit(solution)/shard_map/ppermute | solution.py:18
  23.4 5.5 %collective-permute-start = (s32[25]{0:T(128)S(1)}, s32[25]{0:T(128)S(1)}, u32[]{:S(2)}, u32[]{:S(2)}) collective-permute-start(s32[25]{0:T(128)S(1)} %pad_add_fusion.own.refs_1_.refs_0_), channel_id=1, source_target_pairs={{4,0},{8,4},{12,8},{16,12},{20,16},{24,20},{28,24},{5,1},{9,5},{13... | collective-permute-start | bytes 308 | tf_op jit(solution)/shard_map/ppermute | solution.py:24
  24.7 7.0 %collective-permute-start.1 = (s32[25]{0:T(128)S(1)}, s32[25]{0:T(128)S(1)}, u32[]{:S(2)}, u32[]{:S(2)}) collective-permute-start(s32[25]{0:T(128)S(1)} %pad_add_fusion.own.refs_1_.refs_0_), channel_id=1, source_target_pairs={{8,0},{12,4},{16,8},{20,12},{24,16},{28,20},{9,1},{13,5},{17,9},{2... | collective-permute-start | bytes 308 | tf_op jit(solution)/shard_map/ppermute | solution.py:24
  32.4 7.6 %collective-permute-start.5 = (f32[16,512]{1,0:T(8,128)S(1)}, f32[16,512]{1,0:T(8,128)S(1)}, u32[]{:S(2)}, u32[]{:S(2)}) collective-permute-start(f32[16,512]{1,0:T(8,128)S(1)} %get-tuple-element.30), channel_id=1, source_target_pairs={{0,4},{4,8},{8,12},{12,16},{16,20},{20,24},{24,28},{1,5},{5,9},{9,... | collective-permute-start | bytes 98312 | tf_op jit(solution)/shard_map/ppermute | solution.py:24
  35.4 4.6 %collective-permute-start.6 = (f32[16,512]{1,0:T(8,128)S(1)}, f32[16,512]{1,0:T(8,128)S(1)}, u32[]{:S(2)}, u32[]{:S(2)}) collective-permute-start(f32[16,512]{1,0:T(8,128)S(1)} %get-tuple-element.31), channel_id=1, source_target_pairs={{0,8},{4,12},{8,16},{12,20},{16,24},{20,28},{1,9},{5,13},{9,17},{1... | collective-permute-start | bytes 98312 | tf_op jit(solution)/shard_map/ppermute | solution.py:24
  38.5 4.9 %collective-permute-start.9 = (f32[8,1024]{1,0:T(8,128)S(1)}, f32[8,1024]{1,0:T(8,128)S(1)}, u32[]{:S(2)}, u32[]{:S(2)}) collective-permute-start(f32[8,1024]{1,0:T(8,128)S(1)} %pad_maximum_fusion.1), channel_id=1, source_target_pairs={{0,16},{4,20},{8,24},{12,28},{16,0},{20,4},{24,8},{28,12},{1,17},{... | collective-permute-start | bytes 98312 | tf_op jit(solution)/shard_map/ppermute | solution.py:18
  44.5 1.2 %collective-permute-start.10 = (f32[8,128]{1,0:T(8,128)S(1)}, f32[8,128]{1,0:T(8,128)S(1)}, u32[]{:S(2)}, u32[]{:S(2)}) collective-permute-start(f32[8,128]{1,0:T(8,128)S(1)} %get-tuple-element.33), channel_id=1, source_target_pairs={{0,1},{1,0},{2,3},{3,2},{4,5},{5,4},{6,7},{7,6},{8,9},{9,8},{10,11... | collective-permute-start | bytes 12296 | tf_op jit(solution)/shard_map/ppermute | solution.py:18
  45.7 3.6 %collective-permute-start.11 = (f32[8,128]{1,0:T(8,128)S(1)}, f32[8,128]{1,0:T(8,128)S(1)}, u32[]{:S(2)}, u32[]{:S(2)}) collective-permute-start(f32[8,128]{1,0:T(8,128)S(1)} %add.18.refs_1_), channel_id=1, source_target_pairs={{0,2},{1,3},{2,0},{3,1},{4,6},{5,7},{6,4},{7,5},{8,10},{9,11},{10,... | collective-permute-start | bytes 12296 | tf_op jit(solution)/shard_map/ppermute | solution.py:18
  50.1 3.8 %collective-permute-start.14 = (f32[4,1024]{1,0:T(4,128)S(1)}, f32[4,1024]{1,0:T(4,128)S(1)}, u32[]{:S(2)}, u32[]{:S(2)}) collective-permute-start(f32[4,1024]{1,0:T(4,128)S(1)} %get-tuple-element.36.refs_13_), channel_id=1, source_target_pairs={{0,4},{4,0},{8,12},{12,8},{16,20},{20,16},{24,28},{28,24},{1,5},{5... | collective-permute-start | bytes 49160 | tf_op jit(solution)/shard_map/ppermute | solution.py:18
  53.9 4.0 %collective-permute-start.15 = (f32[8,1024]{1,0:T(8,128)S(1)}, f32[8,1024]{1,0:T(8,128)S(1)}, u32[]{:S(2)}, u32[]{:S(2)}) collective-permute-start(f32[8,1024]{1,0:T(8,128)S(1)} %pad_maximum_fusion.2), channel_id=1, source_target_pairs={{0,8},{4,12},{8,0},{12,4},{16,24},{20,28},{24,16},{28,20},{1,9},{5... | collective-permute-start | bytes 98312 | tf_op jit(solution)/shard_map/ppermute | solution.py:18
  57.9 9.0 %collective-permute-start.16 = (f32[16,1024]{1,0:T(8,128)S(1)}, f32[16,1024]{1,0:T(8,128)S(1)}, u32[]{:S(2)}, u32[]{:S(2)}) collective-permute-start(f32[16,1024]{1,0:T(8,128)S(1)} %pad_maximum_fusion), channel_id=1, source_target_pairs={{0,16},{4,20},{8,24},{12,28},{16,0},{20,4},{24,8},{28,12},{1,17},{... | collective-permute-start | bytes 196616 | tf_op jit(solution)/shard_map/ppermute | solution.py:18
  59.4 5.6 %collective-permute-start.12 = (f32[8,512]{1,0:T(8,128)S(1)}, f32[8,512]{1,0:T(8,128)S(1)}, u32[]{:S(2)}, u32[]{:S(2)}) collective-permute-start(f32[8,512]{1,0:T(8,128)S(1)} %get-tuple-element.35.refs_4_), channel_id=1, source_target_pairs={{4,0},{8,4},{12,8},{16,12},{20,16},{24,20},{28,24},{5,1},{9,5},{13... | collective-permute-start | bytes 49160 | tf_op jit(solution)/shard_map/ppermute | solution.py:24
  60.7 6.2 %collective-permute-start.13 = (f32[8,512]{1,0:T(8,128)S(1)}, f32[8,512]{1,0:T(8,128)S(1)}, u32[]{:S(2)}, u32[]{:S(2)}) collective-permute-start(f32[8,512]{1,0:T(8,128)S(1)} %get-tuple-element.35.refs_4_), channel_id=1, source_target_pairs={{8,0},{12,4},{16,8},{20,12},{24,16},{28,20},{9,1},{13,5},{17,9},{2... | collective-permute-start | bytes 49160 | tf_op jit(solution)/shard_map/ppermute | solution.py:24
  68.3 11.1 %copy-start = (f32[128,1024]{1,0:T(8,128)S(1)}, f32[128,1024]{1,0:T(8,128)}, u32[]{:S(2)}) copy-start(f32[128,1024]{1,0:T(8,128)} %direction_ref.3) | copy-start | bytes 1572868
  68.3 11.1 %copy-start.2 = (f32[128,1024]{1,0:T(8,128)S(1)}, f32[128,1024]{1,0:T(8,128)}, u32[]{:S(2)}) copy-start(f32[128,1024]{1,0:T(8,128)} %residual_ref.3) | copy-start | bytes 1572868
  68.3 6.4 %collective-permute-start.17 = (bf16[128,1024]{1,0:T(8,128)(2,1)S(1)}, bf16[128,1024]{1,0:T(8,128)(2,1)S(1)}, u32[]{:S(2)}, u32[]{:S(2)}) collective-permute-start(bf16[128,1024]{1,0:T(8,128)(2,1)S(1)} %shard_map.136.a_ref), channel_id=1, source_target_pairs={{0,2},{1,3},{2,0},{3,1},{4,6},{5,7},{6,4},{7,5},{8,10},{9,11},{10,... | collective-permute-start | bytes 786440 | tf_op jit(solution)/shard_map/ppermute | solution.py:18
  69.9 4.9 %collective-permute-start.19 = (bf16[128,1024]{1,0:T(8,128)(2,1)S(1)}, bf16[128,1024]{1,0:T(8,128)(2,1)S(1)}, u32[]{:S(2)}, u32[]{:S(2)}) collective-permute-start(bf16[128,1024]{1,0:T(8,128)(2,1)S(1)} %shard_map.136.a_ref), channel_id=1, source_target_pairs={{0,1},{1,0},{2,3},{3,2},{4,5},{5,4},{6,7},{7,6},{8,9},{9,8},{10,11... | collective-permute-start | bytes 786440 | tf_op jit(solution)/shard_map/ppermute | solution.py:18
  74.7 4.7 %collective-permute-start.18 = (bf16[128,1024]{1,0:T(8,128)(2,1)S(1)}, bf16[128,1024]{1,0:T(8,128)(2,1)S(1)}, u32[]{:S(2)}, u32[]{:S(2)}) collective-permute-start(bf16[128,1024]{1,0:T(8,128)(2,1)S(1)} %collective-permute-done.17.a_ref), channel_id=1, source_target_pairs={{0,1},{1,0},{2,3},{3,2},{4,5},{5,4},{6,7},{7,6},{8,9},{9,8},{10,11... | collective-permute-start | bytes 786440 | tf_op jit(solution)/shard_map/ppermute | solution.py:18
  78.5 18.6 %copy-start.3 = (f32[128,1024]{1,0:T(8,128)S(1)}, f32[128,1024]{1,0:T(8,128)}, u32[]{:S(2)}) copy-start(f32[128,1024]{1,0:T(8,128)} %solution_ref.1) | copy-start | bytes 1572868
  80.4 1.3 %collective-permute-start.20 = (f32[8,128]{1,0:T(8,128)S(1)}, f32[8,128]{1,0:T(8,128)S(1)}, u32[]{:S(2)}, u32[]{:S(2)}) collective-permute-start(f32[8,128]{1,0:T(8,128)S(1)} %get-tuple-element.39), channel_id=1, source_target_pairs={{0,1},{1,0},{2,3},{3,2},{4,5},{5,4},{6,7},{7,6},{8,9},{9,8},{10,11... | collective-permute-start | bytes 12296 | tf_op jit(solution)/shard_map/ppermute | solution.py:18
  81.8 3.6 %collective-permute-start.21 = (f32[8,128]{1,0:T(8,128)S(1)}, f32[8,128]{1,0:T(8,128)S(1)}, u32[]{:S(2)}, u32[]{:S(2)}) collective-permute-start(f32[8,128]{1,0:T(8,128)S(1)} %add.19), channel_id=1, source_target_pairs={{0,2},{1,3},{2,0},{3,1},{4,6},{5,7},{6,4},{7,5},{8,10},{9,11},{10,... | collective-permute-start | bytes 12296 | tf_op jit(solution)/shard_map/ppermute | solution.py:18
  85.4 3.6 %collective-permute-start.22 = (f32[8,128]{1,0:T(8,128)S(1)}, f32[8,128]{1,0:T(8,128)S(1)}, u32[]{:S(2)}, u32[]{:S(2)}) collective-permute-start(f32[8,128]{1,0:T(8,128)S(1)} %add.20), channel_id=1, source_target_pairs={{0,4},{4,0},{8,12},{12,8},{16,20},{20,16},{24,28},{28,24},{1,5},{5... | collective-permute-start | bytes 12296 | tf_op jit(solution)/shard_map/ppermute | solution.py:18
  89.0 3.6 %collective-permute-start.23 = (f32[8,128]{1,0:T(8,128)S(1)}, f32[8,128]{1,0:T(8,128)S(1)}, u32[]{:S(2)}, u32[]{:S(2)}) collective-permute-start(f32[8,128]{1,0:T(8,128)S(1)} %add.21), channel_id=1, source_target_pairs={{0,8},{4,12},{8,0},{12,4},{16,24},{20,28},{24,16},{28,20},{1,9},{5... | collective-permute-start | bytes 12296 | tf_op jit(solution)/shard_map/ppermute | solution.py:18
  92.6 4.5 %collective-permute-start.24 = (f32[8,128]{1,0:T(8,128)S(1)}, f32[8,128]{1,0:T(8,128)S(1)}, u32[]{:S(2)}, u32[]{:S(2)}) collective-permute-start(f32[8,128]{1,0:T(8,128)S(1)} %add.22), channel_id=1, source_target_pairs={{0,16},{4,20},{8,24},{12,28},{16,0},{20,4},{24,8},{28,12},{1,17},{... | collective-permute-start | bytes 12296 | tf_op jit(solution)/shard_map/ppermute | solution.py:18
where the time goes:
time: 98.8 us; the launch traced here: 98.5 us
  waiting for transfers between devices  42.1 us (43%)
  starting transfers between devices  36.2 us (37%)
  Pallas kernels  17.4 us (18%)
  between operations  1.54 us (2%)
  other arithmetic  1.22 us (1%)
    ppermute x19, waiting for transfers between devices, swapped(): lax.ppermute(block, axis, [(i, i ^ bit) for i in range(lax.axis_size(axis...  31.5 us
    ppermute x19, starting transfers between devices, swapped(): lax.ppermute(block, axis, [(i, i ^ bit) for i in range(lax.axis_size(axis...  25 us
    pallas_call x11, Pallas kernels, on_chip(): call(*scalars, *arrays, *(pltpu.with_memory_space_constraint(a, pltpu.HBM...  17.4 us
    ppermute x6, starting transfers between devices, shifted(): return lax.ppermute(block, axis, route)  11.2 us
    ppermute x6, waiting for transfers between devices, shifted(): return lax.ppermute(block, axis, route)  10.7 us
  transfers between devices with their start and end apart: 25, of which 17 were waited for; matrix products, arithmetic and copies ran while one was open for 0% of the time, Pallas kernels for 11%

commit v1 on v0

--- a/solution.py
+++ b/solution.py
@@ -74,7 +74,7 @@
 
 
 def slots_of(place):
-    return (place.shape[0] - 1) // 3
+    return place.shape[0] // 4
 
 
 def tile_at(place, slot, steps):
@@ -245,7 +245,6 @@
         return piece_row(ends, 2, window ^ own, 0) * state + piece_row(ends, 2, window ^ own, 1)
 
     lax.fori_loop(0, windows, one, jnp.zeros((1, width), jnp.float32), unroll=windows <= 8)
-    live = place[3 * capacity]
     for slot in range(capacity):
         which, _, first = tile_at(place, slot, steps)
         columns = pl.ds(pl.multiple_of(first * LANES, FB), FB)
@@ -258,7 +257,7 @@
         )
         factor_ref[row, :] = factor
         value = offset + factor * entered[pl.ds(which, 1), columns]
-        picked[row, :] = jnp.where(slot < live, value, 0.0)
+        picked[row, :] = jnp.where(place[3 * capacity + slot] == 1, value, 0.0)
     rows = picked[...].astype(jnp.bfloat16)
     products = nt_dot(rows, tiles_ref[...].reshape(capacity * soundings, cells))
     blocks = lax.broadcasted_iota(jnp.int32, seen_ref.shape, 0)
@@ -276,11 +275,10 @@
     observed = seen_ref[...] + other_ref[...]
     weights[...] = (observed * noise_ref[...]).astype(jnp.bfloat16).astype(jnp.float32)
     slots = lax.broadcasted_iota(jnp.int32, (capacity, soundings), 0)
-    live = place[3 * capacity]
     pieces = []
     for slot in range(capacity):
         picked = weights[pl.ds(place[2 * capacity + slot], 1), :]
-        pieces.append(jnp.where((slots == slot) & (slot < live), picked, 0.0))
+        pieces.append(jnp.where((slots == slot) & (place[3 * capacity + slot] == 1), picked, 0.0))
     spread = jnp.concatenate(pieces, axis=1).astype(jnp.bfloat16)
     rows = jnp.dot(
         spread,
@@ -325,10 +323,9 @@
     )
     terms[...] = jnp.zeros_like(terms)
     for reader, (place, rows) in enumerate(((own, own_ref), (near, near_ref), (far, far_ref))):
-        live = place[3 * capacity]
         for slot in range(capacity):
             which, step, first = tile_at(place, slot, steps)
-            mine = (which == BACK - reader) & (slot < live)
+            mine = (which == BACK - reader) & (place[3 * capacity + slot] == 1)
             step = pl.ds(step, 1)
             for k in range(FB // LANES):
                 terms[first + k, step, :] = terms[first + k, step, :] + jnp.where(
@@ -369,17 +366,22 @@
         image_ref[:, at] = image
         terms = (residual * residual, direction * image, residual * image, image * image)
         totals = [t + jnp.sum(term, axis=0, keepdims=True) for t, term in zip(totals, terms)]
-    sums_ref[...] = jnp.zeros_like(sums_ref)
+    lane = lax.broadcasted_iota(jnp.int32, (1, LANES), 1)
+    row = jnp.zeros((1, LANES), jnp.float32)
     for k, total in enumerate(totals):
-        sums_ref[k : k + 1, :] = jnp.broadcast_to(
-            jnp.sum(total, axis=1, keepdims=True), (1, LANES)
-        )
+        row = jnp.where(lane == k, jnp.sum(total, axis=1, keepdims=True), row)
+    for device in range(sums_ref.shape[0]):
+        sums_ref[device] = row
 
 
 def update_kernel(
     totals_ref, solution_ref, residual_ref, direction_ref, image_ref, solution_new, residual_new, direction_new
 ):
-    norm_old, curvature, cross_sum, image_sq = (totals_ref[k : k + 1, :] for k in range(4))
+    lane = lax.broadcasted_iota(jnp.int32, (1, LANES), 1)
+    total = jnp.sum(totals_ref[...], axis=0)
+    norm_old, curvature, cross_sum, image_sq = (
+        jnp.sum(jnp.where(lane == k, total, 0.0), axis=1, keepdims=True) for k in range(4)
+    )
     step_len = norm_old / curvature
     norm_new = norm_old - 2.0 * step_len * cross_sum + step_len * step_len * image_sq
     ratio = norm_new / norm_old
@@ -413,8 +415,10 @@
     f32 = jnp.float32
     columns = pltpu.VMEM((width // LANES, steps, LANES), f32)
     regions = spatial.shape[1] // width
-
-    place = jnp.concatenate([tile_time[0, 0], tile_cell[0, 0], tile_block[0, 0], tile_count[0]])
+    devices = lax.axis_size("tm") * lax.axis_size("region")
+
+    live = (jnp.arange(capacity, dtype=jnp.int32)[None] < tile_count).astype(jnp.int32)
+    place = jnp.concatenate([tile_time[0], tile_cell[0], tile_block[0], live], axis=1)[0]
     half = direction.astype(jnp.bfloat16)
     blocks = region_blocks(half)
     part, prefix, decays, gains, last, kept = on_chip(
@@ -482,13 +486,9 @@
         image_kernel,
         [region],
         [blocks[3], kept, part, direction, residual],
-        [((steps, width), f32), ((SUB, LANES), f32)],
-    )
-    for axis in ("region", "tm"):
-        bit = 1
-        while bit < lax.axis_size(axis):
-            totals = totals + swapped(totals, axis, bit)
-            bit *= 2
+        [((steps, width), f32), ((devices, 1, LANES), f32)],
+    )
+    totals = lax.all_to_all(totals, ("tm", "region"), 0, 0, tiled=True)
     return on_chip(
         update_kernel,
         [],

time: 98.8 us -> 94.2 us (0.953)
  blocking collectives: 0 us -> 11.4 us
  starting transfers between devices: 36.2 us -> 28 us
  waiting for transfers between devices: 42.1 us -> 34.2 us
    all_to_all x0 -> x1, blocking collectives: none -> 11.4 us  [body(): totals = lax.all_to_all(totals, ('tm', 'region'), 0, 0, tiled=True)]
    ppermute x19 -> x14, starting transfers between devices: 25 us -> 16.8 us  [swapped(): lax.ppermute(block, axis, [(i, i ^ bit) for i in range(lax.axis_size(axis...]
    ppermute x19 -> x14, waiting for transfers between devices: 31.5 us -> 23.5 us  [swapped(): lax.ppermute(block, axis, [(i, i ^ bit) for i in range(lax.axis_size(axis...]
  transfers between devices with their start and end apart: 25 -> 20, of which waited for: 17 -> 12; matrix products, arithmetic and copies ran while one was open for 0% -> 0% of each run, Pallas kernels for 11% -> 11%
where the time goes in v1:
time: 94.2 us; the launch traced here: 93.9 us
  waiting for transfers between devices  34.2 us (36%)
  starting transfers between devices  28 us (30%)
  Pallas kernels  17.5 us (19%)
  blocking collectives  11.4 us (12%)
  between operations  1.55 us (2%)
  other arithmetic  1.21 us (1%)
    ppermute x14, waiting for transfers between devices, swapped(): lax.ppermute(block, axis, [(i, i ^ bit) for i in range(lax.axis_size(axis...  23.5 us
    pallas_call x11, Pallas kernels, on_chip(): call(*scalars, *arrays, *(pltpu.with_memory_space_constraint(a, pltpu.HBM...  17.5 us
    ppermute x14, starting transfers between devices, swapped(): lax.ppermute(block, axis, [(i, i ^ bit) for i in range(lax.axis_size(axis...  16.8 us
    all_to_all x1, blocking collectives, body(): totals = lax.all_to_all(totals, ('tm', 'region'), 0, 0, tiled=True)  11.4 us
    ppermute x6, starting transfers between devices, shifted(): return lax.ppermute(block, axis, route)  11.2 us
    ppermute x6, waiting for transfers between devices, shifted(): return lax.ppermute(block, axis, route)  10.7 us
  transfers between devices with their start and end apart: 20, of which 12 were waited for; matrix products, arithmetic and copies ran while one was open for 0% of the time, Pallas kernels for 11%

profile of v1, /device:TPU:0, one launch (start us, length us, event | category | flops | bytes accessed | tf_op | source)
XLA Modules:
  0.0 93.9 jit_solution(9095463906658198622)
XLA Ops:
  0.6 1.1 %convert_element_type.15.a_ref = bf16[128,1024]{1,0:T(8,128)(2,1)S(1)} convert(f32[128,1024]{1,0:T(8,128)} %direction_ref.3) | non-fusion elementwise | flops 131072 | bytes 786432 | tf_op jit(solution)/shard_map/convert_element_type | solution.py:422
  1.7 3.1 %collective-permute-start.2 = (bf16[128,1024]{1,0:T(8,128)(2,1)S(1)}, bf16[128,1024]{1,0:T(8,128)(2,1)S(1)}, u32[]{:S(2)}, u32[]{:S(2)}) collective-permute-start(bf16[128,1024]{1,0:T(8,128)(2,1)S(1)} %convert_element_type.15.a_ref), channel_id=1, source_target_pairs={{0,2},{1,3},{2,0},{3,1},{4,6},{5,7},{6,4},{7,5},{8,10},{9,11},{10,... | collective-permute-start | bytes 786440 | tf_op jit(solution)/shard_map/ppermute | solution.py:18
  4.8 0.0 collective-permute-start.4
  4.8 6.3 %collective-permute-done.2.a_ref = bf16[128,1024]{1,0:T(8,128)(2,1)S(1)} collective-permute-done((bf16[128,1024]{1,0:T(8,128)(2,1)S(1)}, bf16[128,1024]{1,0:T(8,128)(2,1)S(1)}, u32[]{:S(2)}, u32[]{:S(2)}) %collective-permute-start.2) | collective-permute-done | bytes 262176 | tf_op jit(solution)/shard_map/ppermute | solution.py:18
  11.1 0.0 collective-permute-start.3
  11.7 0.0 collective-permute-done.4.b_ref
  11.7 4.6 %shard_map.130 = (f32[128,1024]{1,0:T(8,128)S(1)}, f32[8,128,128]{2,1,0:T(8,128)S(1)}, f32[8,128,128]{2,1,0:T(8,128)S(1)}, f32[8,128,128]{2,1,0:T(8,128)S(1)}, f...) custom-call(s32[1]{0:T(128)} %bitcast.region, bf16[128,1024]{1,0:T(8,128)(2,1)S(1)} %convert_element_type.15.a_ref, ...), custom_call_target="tpu_custom_call" | custom-call | tf_op jit(solution)/shard_map/pallas_call | solution.py:69
  16.4 0.0 copy-start.5
  16.4 0.0 copy-start.6
  16.4 0.0 copy-start.7
  16.4 0.0 copy-start.1
  16.4 0.8 shard_map.131.part_ref
  17.3 0.0 copy-start.4
  17.3 0.0 collective-permute-done.3.b_ref
  17.3 1.1 %shard_map.132 = (f32[8,128,128]{2,1,0:T(8,128)S(1)}, f32[2,1024]{1,0:T(2,128)S(1)}) custom-call(s32[1]{0:T(128)} %bitcast.region, bf16[128,1024]{1,0:T(8,128)(2,1)S(1)} %collective-permute-done.3.b_ref, bf16[1024,4096]{1,0:T(8,128)(2,1)S(1)} %get-tuple-element.22.spatial, f32[128,1024]{1,0:T(8,128)S(1)} %shard_map.131.part_ref, ...), custom_call_target="tpu_custom_call" | custom-call | tf_op jit(solution)/shard_map/pallas_call | solution.py:69
  18.4 1.8 %collective-permute-start.7 = (f32[2,1024]{1,0:T(2,128)S(1)}, f32[2,1024]{1,0:T(2,128)S(1)}, u32[]{:S(2)}, u32[]{:S(2)}) collective-permute-start(f32[2,1024]{1,0:T(2,128)S(1)} %get-tuple-element.32.refs_6_.refs_9_), channel_id=1, source_target_pairs={{0,4},{4,0},{8,12},{12,8},{16,20},{20,16},{24,28},{28,24},{1,5},{5... | collective-permute-start | bytes 24584 | tf_op jit(solution)/shard_map/ppermute | solution.py:18
  20.2 1.9 %collective-permute-done.7.refs_7_.refs_10_ = f32[2,1024]{1,0:T(2,128)S(1)} collective-permute-done((f32[2,1024]{1,0:T(2,128)S(1)}, f32[2,1024]{1,0:T(2,128)S(1)}, u32[]{:S(2)}, u32[]{:S(2)}) %collective-permute-start.7) | collective-permute-done | bytes 8224 | tf_op jit(solution)/shard_map/ppermute | solution.py:18
  22.1 1.9 %collective-permute-start.8 = (f32[4,1024]{1,0:T(4,128)S(1)}, f32[4,1024]{1,0:T(4,128)S(1)}, u32[]{:S(2)}, u32[]{:S(2)}) collective-permute-start(f32[4,1024]{1,0:T(4,128)S(1)} %pad_maximum_fusion.3), channel_id=1, source_target_pairs={{0,8},{4,12},{8,0},{12,4},{16,24},{20,28},{24,16},{28,20},{1,9},{5... | collective-permute-start | bytes 49160 | tf_op jit(solution)/shard_map/ppermute | solution.py:18
  24.0 0.0 copy-done.5
  24.0 0.0 copy-done.7
  24.0 0.1 add_bitcast_fusion.own.refs_1_.refs_0_
  24.1 1.3 %collective-permute-start = (s32[32]{0:T(128)S(1)}, s32[32]{0:T(128)S(1)}, u32[]{:S(2)}, u32[]{:S(2)}) collective-permute-start(s32[32]{0:T(128)S(1)} %add_bitcast_fusion.own.refs_1_.refs_0_), channel_id=1, source_target_pairs={{4,0},{8,4},{12,8},{16,12},{20,16},{24,20},{28,24},{5,1},{9,5},{13... | collective-permute-start | bytes 392 | tf_op jit(solution)/shard_map/ppermute | solution.py:24
  25.3 1.3 %collective-permute-start.1 = (s32[32]{0:T(128)S(1)}, s32[32]{0:T(128)S(1)}, u32[]{:S(2)}, u32[]{:S(2)}) collective-permute-start(s32[32]{0:T(128)S(1)} %add_bitcast_fusion.own.refs_1_.refs_0_), channel_id=1, source_target_pairs={{8,0},{12,4},{16,8},{20,12},{24,16},{28,20},{9,1},{13,5},{17,9},{2... | collective-permute-start | bytes 392 | tf_op jit(solution)/shard_map/ppermute | solution.py:24
  26.6 2.9 %collective-permute-done.near.refs_2_ = s32[32]{0:T(128)S(1)} collective-permute-done((s32[32]{0:T(128)S(1)}, s32[32]{0:T(128)S(1)}, u32[]{:S(2)}, u32[]{:S(2)}) %collective-permute-start) | collective-permute-done | bytes 160 | tf_op jit(solution)/shard_map/ppermute | solution.py:24
  29.5 2.9 %collective-permute-done.1.far.refs_3_ = s32[32]{0:T(128)S(1)} collective-permute-done((s32[32]{0:T(128)S(1)}, s32[32]{0:T(128)S(1)}, u32[]{:S(2)}, u32[]{:S(2)}) %collective-permute-start.1) | collective-permute-done | bytes 160 | tf_op jit(solution)/shard_map/ppermute | solution.py:24
  32.4 0.7 shard_map.133
  33.0 3.0 %collective-permute-start.5 = (f32[16,512]{1,0:T(8,128)S(1)}, f32[16,512]{1,0:T(8,128)S(1)}, u32[]{:S(2)}, u32[]{:S(2)}) collective-permute-start(f32[16,512]{1,0:T(8,128)S(1)} %get-tuple-element.30), channel_id=1, source_target_pairs={{0,4},{4,8},{8,12},{12,16},{16,20},{20,24},{24,28},{1,5},{5,9},{9,... | collective-permute-start | bytes 98312 | tf_op jit(solution)/shard_map/ppermute | solution.py:24
  36.0 3.0 %collective-permute-start.6 = (f32[16,512]{1,0:T(8,128)S(1)}, f32[16,512]{1,0:T(8,128)S(1)}, u32[]{:S(2)}, u32[]{:S(2)}) collective-permute-start(f32[16,512]{1,0:T(8,128)S(1)} %get-tuple-element.31), channel_id=1, source_target_pairs={{0,8},{4,12},{8,16},{12,20},{16,24},{20,28},{1,9},{5,13},{9,17},{1... | collective-permute-start | bytes 98312 | tf_op jit(solution)/shard_map/ppermute | solution.py:24
  39.1 0.0 collective-permute-done.8.refs_8_.refs_11_
  39.1 1.5 %collective-permute-start.9 = (f32[8,1024]{1,0:T(8,128)S(1)}, f32[8,1024]{1,0:T(8,128)S(1)}, u32[]{:S(2)}, u32[]{:S(2)}) collective-permute-start(f32[8,1024]{1,0:T(8,128)S(1)} %pad_maximum_fusion.1), channel_id=1, source_target_pairs={{0,16},{4,20},{8,24},{12,28},{16,0},{20,4},{24,8},{28,12},{1,17},{... | collective-permute-start | bytes 98312 | tf_op jit(solution)/shard_map/ppermute | solution.py:18
  40.7 0.0 collective-permute-done.5.refs_3_
  40.7 0.0 collective-permute-done.6.refs_4_
  40.7 3.3 %collective-permute-done.9.refs_9_.refs_12_ = f32[8,1024]{1,0:T(8,128)S(1)} collective-permute-done((f32[8,1024]{1,0:T(8,128)S(1)}, f32[8,1024]{1,0:T(8,128)S(1)}, u32[]{:S(2)}, u32[]{:S(2)}) %collective-permute-start.9) | collective-permute-done | bytes 32800 | tf_op jit(solution)/shard_map/ppermute | solution.py:18
  44.0 1.1 %shard_map.134 = (f32[8,128]{1,0:T(8,128)S(1)}, f32[8,512]{1,0:T(8,128)S(1)}) custom-call(s32[1]{0:T(128)} %bitcast.1.refs_0_, s32[32]{0:T(128)S(1)} %add_bitcast_fusion.own.refs_1_.refs_0_, f32[16,512]{1,0:T(8,128)S(1)} %get-tuple-element.29.refs_2_, f32[16,512]{1,0:T(8,128)S(1)} %collective-permute-done.5.refs_3_, ...), custom_call_target="tpu_custom_call" | custom-call | tf_op jit(solution)/shard_map/pallas_call | solution.py:69
  45.1 0.0 collective-permute-start.10
  45.1 1.2 %collective-permute-done.10 = f32[8,128]{1,0:T(8,128)S(1)} collective-permute-done((f32[8,128]{1,0:T(8,128)S(1)}, f32[8,128]{1,0:T(8,128)S(1)}, u32[]{:S(2)}, u32[]{:S(2)}) %collective-permute-start.10) | collective-permute-done | bytes 4128 | tf_op jit(solution)/shard_map/ppermute | solution.py:18
  46.3 1.5 %collective-permute-start.11 = (f32[8,128]{1,0:T(8,128)S(1)}, f32[8,128]{1,0:T(8,128)S(1)}, u32[]{:S(2)}, u32[]{:S(2)}) collective-permute-start(f32[8,128]{1,0:T(8,128)S(1)} %add.3.refs_1_), channel_id=1, source_target_pairs={{0,2},{1,3},{2,0},{3,1},{4,6},{5,7},{6,4},{7,5},{8,10},{9,11},{10,... | collective-permute-start | bytes 12296 | tf_op jit(solution)/shard_map/ppermute | solution.py:18
  47.8 2.1 %collective-permute-done.11.refs_2_ = f32[8,128]{1,0:T(8,128)S(1)} collective-permute-done((f32[8,128]{1,0:T(8,128)S(1)}, f32[8,128]{1,0:T(8,128)S(1)}, u32[]{:S(2)}, u32[]{:S(2)}) %collective-permute-start.11) | collective-permute-done | bytes 4128 | tf_op jit(solution)/shard_map/ppermute | solution.py:18
  49.9 0.8 shard_map.135
  50.8 1.9 %collective-permute-start.14 = (f32[4,1024]{1,0:T(4,128)S(1)}, f32[4,1024]{1,0:T(4,128)S(1)}, u32[]{:S(2)}, u32[]{:S(2)}) collective-permute-start(f32[4,1024]{1,0:T(4,128)S(1)} %get-tuple-element.36.refs_13_), channel_id=1, source_target_pairs={{0,4},{4,0},{8,12},{12,8},{16,20},{20,16},{24,28},{28,24},{1,5},{5... | collective-permute-start | bytes 49160 | tf_op jit(solution)/shard_map/ppermute | solution.py:18
  52.6 1.9 %collective-permute-done.14.refs_14_ = f32[4,1024]{1,0:T(4,128)S(1)} collective-permute-done((f32[4,1024]{1,0:T(4,128)S(1)}, f32[4,1024]{1,0:T(4,128)S(1)}, u32[]{:S(2)}, u32[]{:S(2)}) %collective-permute-start.14) | collective-permute-done | bytes 16416 | tf_op jit(solution)/shard_map/ppermute | solution.py:18
  54.6 2.1 %collective-permute-start.15 = (f32[8,1024]{1,0:T(8,128)S(1)}, f32[8,1024]{1,0:T(8,128)S(1)}, u32[]{:S(2)}, u32[]{:S(2)}) collective-permute-start(f32[8,1024]{1,0:T(8,128)S(1)} %pad_maximum_fusion.2), channel_id=1, source_target_pairs={{0,8},{4,12},{8,0},{12,4},{16,24},{20,28},{24,16},{28,20},{1,9},{5... | collective-permute-start | bytes 98312 | tf_op jit(solution)/shard_map/ppermute | solution.py:18
  56.6 1.9 %collective-permute-done.15.refs_15_ = f32[8,1024]{1,0:T(8,128)S(1)} collective-permute-done((f32[8,1024]{1,0:T(8,128)S(1)}, f32[8,1024]{1,0:T(8,128)S(1)}, u32[]{:S(2)}, u32[]{:S(2)}) %collective-permute-start.15) | collective-permute-done | bytes 32800 | tf_op jit(solution)/shard_map/ppermute | solution.py:18
  58.6 1.5 %collective-permute-start.16 = (f32[16,1024]{1,0:T(8,128)S(1)}, f32[16,1024]{1,0:T(8,128)S(1)}, u32[]{:S(2)}, u32[]{:S(2)}) collective-permute-start(f32[16,1024]{1,0:T(8,128)S(1)} %pad_maximum_fusion), channel_id=1, source_target_pairs={{0,16},{4,20},{8,24},{12,28},{16,0},{20,4},{24,8},{28,12},{1,17},{... | collective-permute-start | bytes 196616 | tf_op jit(solution)/shard_map/ppermute | solution.py:18
  60.1 1.3 %collective-permute-start.12 = (f32[8,512]{1,0:T(8,128)S(1)}, f32[8,512]{1,0:T(8,128)S(1)}, u32[]{:S(2)}, u32[]{:S(2)}) collective-permute-start(f32[8,512]{1,0:T(8,128)S(1)} %get-tuple-element.35.refs_4_), channel_id=1, source_target_pairs={{4,0},{8,4},{12,8},{16,12},{20,16},{24,20},{28,24},{5,1},{9,5},{13... | collective-permute-start | bytes 49160 | tf_op jit(solution)/shard_map/ppermute | solution.py:24
  61.4 1.3 %collective-permute-start.13 = (f32[8,512]{1,0:T(8,128)S(1)}, f32[8,512]{1,0:T(8,128)S(1)}, u32[]{:S(2)}, u32[]{:S(2)}) collective-permute-start(f32[8,512]{1,0:T(8,128)S(1)} %get-tuple-element.35.refs_4_), channel_id=1, source_target_pairs={{8,0},{12,4},{16,8},{20,12},{24,16},{28,20},{9,1},{13,5},{17,9},{2... | collective-permute-start | bytes 49160 | tf_op jit(solution)/shard_map/ppermute | solution.py:24
  62.7 3.0 %collective-permute-done.12.refs_5_ = f32[8,512]{1,0:T(8,128)S(1)} collective-permute-done((f32[8,512]{1,0:T(8,128)S(1)}, f32[8,512]{1,0:T(8,128)S(1)}, u32[]{:S(2)}, u32[]{:S(2)}) %collective-permute-start.12) | collective-permute-done | bytes 16416 | tf_op jit(solution)/shard_map/ppermute | solution.py:24
  65.7 1.9 %collective-permute-done.13.refs_6_ = f32[8,512]{1,0:T(8,128)S(1)} collective-permute-done((f32[8,512]{1,0:T(8,128)S(1)}, f32[8,512]{1,0:T(8,128)S(1)}, u32[]{:S(2)}, u32[]{:S(2)}) %collective-permute-start.13) | collective-permute-done | bytes 16416 | tf_op jit(solution)/shard_map/ppermute | solution.py:24
  67.6 0.0 collective-permute-done.16.refs_16_
  67.6 1.3 %shard_map.136.a_ref = bf16[128,1024]{1,0:T(8,128)(2,1)S(1)} custom-call(s32[1]{0:T(128)} %bitcast.1.refs_0_, s32[32]{0:T(128)S(1)} %add_bitcast_fusion.own.refs_1_.refs_0_, s32[32]{0:T(128)S(1)} %collective-permute-done.near.refs_2_, s32[32]{0:T(128)S(1)} %collective-permute-done.1.far.refs_3_, f32[8,512]{1,0:T(8,128)S(1)} %get-tuple-element.35.refs_4_, ...), custom_call_target="tpu_custom_call" | custom-call | tf_op jit(solution)/shard_map/pallas_call | solution.py:69
  68.9 0.0 copy-start
  69.0 0.0 copy-start.2
  69.0 1.6 %collective-permute-start.17 = (bf16[128,1024]{1,0:T(8,128)(2,1)S(1)}, bf16[128,1024]{1,0:T(8,128)(2,1)S(1)}, u32[]{:S(2)}, u32[]{:S(2)}) collective-permute-start(bf16[128,1024]{1,0:T(8,128)(2,1)S(1)} %shard_map.136.a_ref), channel_id=1, source_target_pairs={{0,2},{1,3},{2,0},{3,1},{4,6},{5,7},{6,4},{7,5},{8,10},{9,11},{10,... | collective-permute-start | bytes 786440 | tf_op jit(solution)/shard_map/ppermute | solution.py:18
  70.6 0.0 collective-permute-start.19
  70.6 4.8 %collective-permute-done.17.a_ref = bf16[128,1024]{1,0:T(8,128)(2,1)S(1)} collective-permute-done((bf16[128,1024]{1,0:T(8,128)(2,1)S(1)}, bf16[128,1024]{1,0:T(8,128)(2,1)S(1)}, u32[]{:S(2)}, u32[]{:S(2)}) %collective-permute-start.17) | collective-permute-done | bytes 262176 | tf_op jit(solution)/shard_map/ppermute | solution.py:18
  75.4 0.0 collective-permute-start.18
  75.4 0.0 collective-permute-done.19.b_ref
  75.4 3.8 %shard_map.137 = (f32[128,1024]{1,0:T(8,128)S(1)}, bf16[1024,4096]{1,0:T(8,128)(2,1)S(1)}) custom-call(s32[1]{0:T(128)} %bitcast.region, bf16[128,1024]{1,0:T(8,128)(2,1)S(1)} %shard_map.136.a_ref, bf16[128,1024]{1,0:T(8,128)(2,1)S(1)} %collective-permute-done.19.b_ref, bf16[1024,4096]{1,0:T(8,128)(2,1)} %spatial_hbm.3), custom_call_target="tpu_custom_call" | custom-call | tf_op jit(solution)/shard_map/pallas_call | solution.py:69
  79.2 0.0 copy-start.3
  79.2 0.8 shard_map.138.part_ref
  80.1 0.0 collective-permute-done.18.b_ref
  80.1 1.0 %shard_map.139 = (f32[128,1024]{1,0:T(8,128)S(1)}, f32[32,1,128]{2,1,0:T(1,128)S(1)}) custom-call(s32[1]{0:T(128)} %bitcast.region, bf16[128,1024]{1,0:T(8,128)(2,1)S(1)} %collective-permute-done.18.b_ref, bf16[1024,4096]{1,0:T(8,128)(2,1)S(1)} %get-tuple-element.37.spatial, f32[128,1024]{1,0:T(8,128)S(1)} %shard_map.138.part_ref, f32[128,1024]{1,0:T(8,128)S(1)} %copy-done, ...), custom_call_target="tpu_custom_call" | custom-call | tf_op jit(solution)/shard_map/pallas_call | solution.py:69
  81.1 11.4 %all_to_all.5.totals_ref = f32[32,1,128]{2,1,0:T(1,128)S(1)} all-to-all(f32[32,1,128]{2,1,0:T(1,128)S(1)} %get-tuple-element.39), channel_id=1, replica_groups=mesh['tm'=8,'region'=4] {'tm','region'}, dimensions={0} | all-to-all | bytes 32768 | tf_op jit(solution)/shard_map/all_to_all | solution.py:491
  92.5 1.4 %shard_map.140 = (f32[128,1024]{1,0:T(8,128)}, f32[128,1024]{1,0:T(8,128)}, f32[128,1024]{1,0:T(8,128)}) custom-call(f32[32,1,128]{2,1,0:T(1,128)S(1)} %all_to_all.5.totals_ref, f32[128,1024]{1,0:T(8,128)S(1)} %copy-done.3, f32[128,1024]{1,0:T(8,128)S(1)} %copy-done.2, f32[128,1024]{1,0:T(8,128)S(1)} %copy-done, f32[128,1024]{1,0:T(8,128)S(1)} %get-tuple-element.40.image_ref), custom_call_target="tpu_custom_call" | custom-call | tf_op jit(solution)/shard_map/pallas_call | solution.py:69
  (12 shorter events, 0.1 us)
Async XLA Ops:
  1.7 9.4 %collective-permute-start.2 = (bf16[128,1024]{1,0:T(8,128)(2,1)S(1)}, bf16[128,1024]{1,0:T(8,128)(2,1)S(1)}, u32[]{:S(2)}, u32[]{:S(2)}) collective-permute-start(bf16[128,1024]{1,0:T(8,128)(2,1)S(1)} %convert_element_type.15.a_ref), channel_id=1, source_target_pairs={{0,2},{1,3},{2,0},{3,1},{4,6},{5,7},{6,4},{7,5},{8,10},{9,11},{10,... | collective-permute-start | bytes 786440 | tf_op jit(solution)/shard_map/ppermute | solution.py:18
  4.8 7.0 %collective-permute-start.4 = (bf16[128,1024]{1,0:T(8,128)(2,1)S(1)}, bf16[128,1024]{1,0:T(8,128)(2,1)S(1)}, u32[]{:S(2)}, u32[]{:S(2)}) collective-permute-start(bf16[128,1024]{1,0:T(8,128)(2,1)S(1)} %convert_element_type.15.a_ref), channel_id=1, source_target_pairs={{0,1},{1,0},{2,3},{3,2},{4,5},{5,4},{6,7},{7,6},{8,9},{9,8},{10,11... | collective-permute-start | bytes 786440 | tf_op jit(solution)/shard_map/ppermute | solution.py:18
  11.1 6.2 %collective-permute-start.3 = (bf16[128,1024]{1,0:T(8,128)(2,1)S(1)}, bf16[128,1024]{1,0:T(8,128)(2,1)S(1)}, u32[]{:S(2)}, u32[]{:S(2)}) collective-permute-start(bf16[128,1024]{1,0:T(8,128)(2,1)S(1)} %collective-permute-done.2.a_ref), channel_id=1, source_target_pairs={{0,1},{1,0},{2,3},{3,2},{4,5},{5,4},{6,7},{7,6},{8,9},{9,8},{10,11... | collective-permute-start | bytes 786440 | tf_op jit(solution)/shard_map/ppermute | solution.py:18
  16.4 7.6 %copy-start.5 = (s32[1,1,8]{2,1,0:T(1,128)S(1)}, s32[1,1,8]{2,1,0:T(1,128)}, u32[]{:S(2)}) copy-start(s32[1,1,8]{2,1,0:T(1,128)} %param.17) | copy-start | bytes 100
  16.4 7.6 %copy-start.6 = (s32[1,1,8]{2,1,0:T(1,128)S(1)}, s32[1,1,8]{2,1,0:T(1,128)}, u32[]{:S(2)}) copy-start(s32[1,1,8]{2,1,0:T(1,128)} %param.19) | copy-start | bytes 100
  16.4 7.6 %copy-start.7 = (s32[1,1,8]{2,1,0:T(1,128)S(1)}, s32[1,1,8]{2,1,0:T(1,128)}, u32[]{:S(2)}) copy-start(s32[1,1,8]{2,1,0:T(1,128)} %param.18) | copy-start | bytes 100
  16.4 27.6 %copy-start.1 = (bf16[1,1,8,128,512]{4,3,2,1,0:T(8,128)(2,1)S(1)}, bf16[1,1,8,128,512]{4,3,2,1,0:T(8,128)(2,1)}, u32[]{:S(2)}) copy-start(bf16[1,1,8,128,512]{4,3,2,1,0:T(8,128)(2,1)} %param.16) | copy-start | bytes 3145732
  17.3 32.7 %copy-start.4 = (f32[8,128]{1,0:T(8,128)S(1)}, f32[8,128]{1,0:T(8,128)}, u32[]{:S(2)}) copy-start(f32[8,128]{1,0:T(8,128)} %refs_3_.1) | copy-start | bytes 12292
  18.4 3.7 %collective-permute-start.7 = (f32[2,1024]{1,0:T(2,128)S(1)}, f32[2,1024]{1,0:T(2,128)S(1)}, u32[]{:S(2)}, u32[]{:S(2)}) collective-permute-start(f32[2,1024]{1,0:T(2,128)S(1)} %get-tuple-element.32.refs_6_.refs_9_), channel_id=1, source_target_pairs={{0,4},{4,0},{8,12},{12,8},{16,20},{20,16},{24,28},{28,24},{1,5},{5... | collective-permute-start | bytes 24584 | tf_op jit(solution)/shard_map/ppermute | solution.py:18
  22.1 17.0 %collective-permute-start.8 = (f32[4,1024]{1,0:T(4,128)S(1)}, f32[4,1024]{1,0:T(4,128)S(1)}, u32[]{:S(2)}, u32[]{:S(2)}) collective-permute-start(f32[4,1024]{1,0:T(4,128)S(1)} %pad_maximum_fusion.3), channel_id=1, source_target_pairs={{0,8},{4,12},{8,0},{12,4},{16,24},{20,28},{24,16},{28,20},{1,9},{5... | collective-permute-start | bytes 49160 | tf_op jit(solution)/shard_map/ppermute | solution.py:18
  24.1 5.5 %collective-permute-start = (s32[32]{0:T(128)S(1)}, s32[32]{0:T(128)S(1)}, u32[]{:S(2)}, u32[]{:S(2)}) collective-permute-start(s32[32]{0:T(128)S(1)} %add_bitcast_fusion.own.refs_1_.refs_0_), channel_id=1, source_target_pairs={{4,0},{8,4},{12,8},{16,12},{20,16},{24,20},{28,24},{5,1},{9,5},{13... | collective-permute-start | bytes 392 | tf_op jit(solution)/shard_map/ppermute | solution.py:24
  25.3 7.0 %collective-permute-start.1 = (s32[32]{0:T(128)S(1)}, s32[32]{0:T(128)S(1)}, u32[]{:S(2)}, u32[]{:S(2)}) collective-permute-start(s32[32]{0:T(128)S(1)} %add_bitcast_fusion.own.refs_1_.refs_0_), channel_id=1, source_target_pairs={{8,0},{12,4},{16,8},{20,12},{24,16},{28,20},{9,1},{13,5},{17,9},{2... | collective-permute-start | bytes 392 | tf_op jit(solution)/shard_map/ppermute | solution.py:24
  33.0 7.6 %collective-permute-start.5 = (f32[16,512]{1,0:T(8,128)S(1)}, f32[16,512]{1,0:T(8,128)S(1)}, u32[]{:S(2)}, u32[]{:S(2)}) collective-permute-start(f32[16,512]{1,0:T(8,128)S(1)} %get-tuple-element.30), channel_id=1, source_target_pairs={{0,4},{4,8},{8,12},{12,16},{16,20},{20,24},{24,28},{1,5},{5,9},{9,... | collective-permute-start | bytes 98312 | tf_op jit(solution)/shard_map/ppermute | solution.py:24
  36.0 4.6 %collective-permute-start.6 = (f32[16,512]{1,0:T(8,128)S(1)}, f32[16,512]{1,0:T(8,128)S(1)}, u32[]{:S(2)}, u32[]{:S(2)}) collective-permute-start(f32[16,512]{1,0:T(8,128)S(1)} %get-tuple-element.31), channel_id=1, source_target_pairs={{0,8},{4,12},{8,16},{12,20},{16,24},{20,28},{1,9},{5,13},{9,17},{1... | collective-permute-start | bytes 98312 | tf_op jit(solution)/shard_map/ppermute | solution.py:24
  39.1 4.9 %collective-permute-start.9 = (f32[8,1024]{1,0:T(8,128)S(1)}, f32[8,1024]{1,0:T(8,128)S(1)}, u32[]{:S(2)}, u32[]{:S(2)}) collective-permute-start(f32[8,1024]{1,0:T(8,128)S(1)} %pad_maximum_fusion.1), channel_id=1, source_target_pairs={{0,16},{4,20},{8,24},{12,28},{16,0},{20,4},{24,8},{28,12},{1,17},{... | collective-permute-start | bytes 98312 | tf_op jit(solution)/shard_map/ppermute | solution.py:18
  45.1 1.2 %collective-permute-start.10 = (f32[8,128]{1,0:T(8,128)S(1)}, f32[8,128]{1,0:T(8,128)S(1)}, u32[]{:S(2)}, u32[]{:S(2)}) collective-permute-start(f32[8,128]{1,0:T(8,128)S(1)} %get-tuple-element.33), channel_id=1, source_target_pairs={{0,1},{1,0},{2,3},{3,2},{4,5},{5,4},{6,7},{7,6},{8,9},{9,8},{10,11... | collective-permute-start | bytes 12296 | tf_op jit(solution)/shard_map/ppermute | solution.py:18
  46.3 3.6 %collective-permute-start.11 = (f32[8,128]{1,0:T(8,128)S(1)}, f32[8,128]{1,0:T(8,128)S(1)}, u32[]{:S(2)}, u32[]{:S(2)}) collective-permute-start(f32[8,128]{1,0:T(8,128)S(1)} %add.3.refs_1_), channel_id=1, source_target_pairs={{0,2},{1,3},{2,0},{3,1},{4,6},{5,7},{6,4},{7,5},{8,10},{9,11},{10,... | collective-permute-start | bytes 12296 | tf_op jit(solution)/shard_map/ppermute | solution.py:18
  50.8 3.8 %collective-permute-start.14 = (f32[4,1024]{1,0:T(4,128)S(1)}, f32[4,1024]{1,0:T(4,128)S(1)}, u32[]{:S(2)}, u32[]{:S(2)}) collective-permute-start(f32[4,1024]{1,0:T(4,128)S(1)} %get-tuple-element.36.refs_13_), channel_id=1, source_target_pairs={{0,4},{4,0},{8,12},{12,8},{16,20},{20,16},{24,28},{28,24},{1,5},{5... | collective-permute-start | bytes 49160 | tf_op jit(solution)/shard_map/ppermute | solution.py:18
  54.6 4.0 %collective-permute-start.15 = (f32[8,1024]{1,0:T(8,128)S(1)}, f32[8,1024]{1,0:T(8,128)S(1)}, u32[]{:S(2)}, u32[]{:S(2)}) collective-permute-start(f32[8,1024]{1,0:T(8,128)S(1)} %pad_maximum_fusion.2), channel_id=1, source_target_pairs={{0,8},{4,12},{8,0},{12,4},{16,24},{20,28},{24,16},{28,20},{1,9},{5... | collective-permute-start | bytes 98312 | tf_op jit(solution)/shard_map/ppermute | solution.py:18
  58.6 9.0 %collective-permute-start.16 = (f32[16,1024]{1,0:T(8,128)S(1)}, f32[16,1024]{1,0:T(8,128)S(1)}, u32[]{:S(2)}, u32[]{:S(2)}) collective-permute-start(f32[16,1024]{1,0:T(8,128)S(1)} %pad_maximum_fusion), channel_id=1, source_target_pairs={{0,16},{4,20},{8,24},{12,28},{16,0},{20,4},{24,8},{28,12},{1,17},{... | collective-permute-start | bytes 196616 | tf_op jit(solution)/shard_map/ppermute | solution.py:18
  60.1 5.6 %collective-permute-start.12 = (f32[8,512]{1,0:T(8,128)S(1)}, f32[8,512]{1,0:T(8,128)S(1)}, u32[]{:S(2)}, u32[]{:S(2)}) collective-permute-start(f32[8,512]{1,0:T(8,128)S(1)} %get-tuple-element.35.refs_4_), channel_id=1, source_target_pairs={{4,0},{8,4},{12,8},{16,12},{20,16},{24,20},{28,24},{5,1},{9,5},{13... | collective-permute-start | bytes 49160 | tf_op jit(solution)/shard_map/ppermute | solution.py:24
  61.4 6.2 %collective-permute-start.13 = (f32[8,512]{1,0:T(8,128)S(1)}, f32[8,512]{1,0:T(8,128)S(1)}, u32[]{:S(2)}, u32[]{:S(2)}) collective-permute-start(f32[8,512]{1,0:T(8,128)S(1)} %get-tuple-element.35.refs_4_), channel_id=1, source_target_pairs={{8,0},{12,4},{16,8},{20,12},{24,16},{28,20},{9,1},{13,5},{17,9},{2... | collective-permute-start | bytes 49160 | tf_op jit(solution)/shard_map/ppermute | solution.py:24
  68.9 11.1 %copy-start = (f32[128,1024]{1,0:T(8,128)S(1)}, f32[128,1024]{1,0:T(8,128)}, u32[]{:S(2)}) copy-start(f32[128,1024]{1,0:T(8,128)} %direction_ref.3) | copy-start | bytes 1572868
  69.0 11.1 %copy-start.2 = (f32[128,1024]{1,0:T(8,128)S(1)}, f32[128,1024]{1,0:T(8,128)}, u32[]{:S(2)}) copy-start(f32[128,1024]{1,0:T(8,128)} %residual_ref.3) | copy-start | bytes 1572868
  69.0 6.4 %collective-permute-start.17 = (bf16[128,1024]{1,0:T(8,128)(2,1)S(1)}, bf16[128,1024]{1,0:T(8,128)(2,1)S(1)}, u32[]{:S(2)}, u32[]{:S(2)}) collective-permute-start(bf16[128,1024]{1,0:T(8,128)(2,1)S(1)} %shard_map.136.a_ref), channel_id=1, source_target_pairs={{0,2},{1,3},{2,0},{3,1},{4,6},{5,7},{6,4},{7,5},{8,10},{9,11},{10,... | collective-permute-start | bytes 786440 | tf_op jit(solution)/shard_map/ppermute | solution.py:18
  70.6 4.9 %collective-permute-start.19 = (bf16[128,1024]{1,0:T(8,128)(2,1)S(1)}, bf16[128,1024]{1,0:T(8,128)(2,1)S(1)}, u32[]{:S(2)}, u32[]{:S(2)}) collective-permute-start(bf16[128,1024]{1,0:T(8,128)(2,1)S(1)} %shard_map.136.a_ref), channel_id=1, source_target_pairs={{0,1},{1,0},{2,3},{3,2},{4,5},{5,4},{6,7},{7,6},{8,9},{9,8},{10,11... | collective-permute-start | bytes 786440 | tf_op jit(solution)/shard_map/ppermute | solution.py:18
  75.4 4.7 %collective-permute-start.18 = (bf16[128,1024]{1,0:T(8,128)(2,1)S(1)}, bf16[128,1024]{1,0:T(8,128)(2,1)S(1)}, u32[]{:S(2)}, u32[]{:S(2)}) collective-permute-start(bf16[128,1024]{1,0:T(8,128)(2,1)S(1)} %collective-permute-done.17.a_ref), channel_id=1, source_target_pairs={{0,1},{1,0},{2,3},{3,2},{4,5},{5,4},{6,7},{7,6},{8,9},{9,8},{10,11... | collective-permute-start | bytes 786440 | tf_op jit(solution)/shard_map/ppermute | solution.py:18
  79.2 13.3 %copy-start.3 = (f32[128,1024]{1,0:T(8,128)S(1)}, f32[128,1024]{1,0:T(8,128)}, u32[]{:S(2)}) copy-start(f32[128,1024]{1,0:T(8,128)} %solution_ref.1) | copy-start | bytes 1572868

commit v2 on v1

--- a/solution.py
+++ b/solution.py
@@ -74,7 +74,7 @@
 
 
 def slots_of(place):
-    return place.shape[0] // 4
+    return (place.shape[0] - 1) // 3
 
 
 def tile_at(place, slot, steps):
@@ -206,10 +206,12 @@
                 local[k, strided(s, steps), :] = states[s] + factors[s] * entering
 
 
-def gather_kernel(own, near, far, local, prefix_ref, own_ref, near_ref, far_ref):
+def gather_kernel(*refs):
+    count = (len(refs) - 2) // 2
+    local, prefix_ref = refs[count : count + 2]
     steps = local.shape[1]
-    capacity = own_ref.shape[0] // 2
-    for place, rows_ref in ((own, own_ref), (near, near_ref), (far, far_ref)):
+    capacity = refs[-1].shape[0] // 2
+    for place, rows_ref in zip(refs[:count], refs[count + 2 :]):
         for slot in range(capacity):
             _, step, first = tile_at(place, slot, steps)
             for k in range(FB // LANES):
@@ -218,22 +220,21 @@
                 rows_ref[capacity + slot : capacity + slot + 1, lanes(k)] = prefix_ref[*at, :]
 
 
-def piece_row(pieces, per, distance, row):
-    found = pieces[0][row : row + 1, :]
-    for k, piece in enumerate(pieces[1:]):
-        inside = jnp.clip(distance - 2**k, 0, 2**k - 1)
-        at = piece[pl.ds(inside * per + row, 1), :]
-        found = jnp.where(distance >= 2**k, at, found)
-    return found
+def lay_out(rows_ref, pieces):
+    at = 0
+    for piece in pieces:
+        rows_ref[at : at + piece.shape[0], :] = piece[...]
+        at += piece.shape[0]
 
 
 def observe_kernel(steps, pieces, here, place, own_ref, near_ref, far_ref, tiles_ref, *rest):
-    ends, (seen_ref, factor_ref, entered, picked) = rest[:pieces], rest[pieces:]
+    ends, (seen_ref, factor_ref, entered, picked, states) = rest[:pieces], rest[pieces:]
     capacity, soundings, cells = tiles_ref.shape
     windows = 2 ** (pieces - 1)
     width = ends[0].shape[1]
     own = here[0]
     entered[...] = jnp.zeros_like(entered)
+    lay_out(states, ends)
 
     def one(window, state):
         for back in range(BACK + 1):
@@ -242,7 +243,8 @@
             def _():
                 entered[BACK - back : BACK - back + 1, :] = state
 
-        return piece_row(ends, 2, window ^ own, 0) * state + piece_row(ends, 2, window ^ own, 1)
+        row = 2 * (window ^ own)
+        return states[pl.ds(row, 1), :] * state + states[pl.ds(row + 1, 1), :]
 
     lax.fori_loop(0, windows, one, jnp.zeros((1, width), jnp.float32), unroll=windows <= 8)
     for slot in range(capacity):
@@ -257,7 +259,7 @@
         )
         factor_ref[row, :] = factor
         value = offset + factor * entered[pl.ds(which, 1), columns]
-        picked[row, :] = jnp.where(place[3 * capacity + slot] == 1, value, 0.0)
+        picked[row, :] = jnp.where(slot < place[3 * capacity], value, 0.0)
     rows = picked[...].astype(jnp.bfloat16)
     products = nt_dot(rows, tiles_ref[...].reshape(capacity * soundings, cells))
     blocks = lax.broadcasted_iota(jnp.int32, seen_ref.shape, 0)
@@ -278,7 +280,7 @@
     pieces = []
     for slot in range(capacity):
         picked = weights[pl.ds(place[2 * capacity + slot], 1), :]
-        pieces.append(jnp.where((slots == slot) & (place[3 * capacity + slot] == 1), picked, 0.0))
+        pieces.append(jnp.where((slots == slot) & (slot < place[3 * capacity]), picked, 0.0))
     spread = jnp.concatenate(pieces, axis=1).astype(jnp.bfloat16)
     rows = jnp.dot(
         spread,
@@ -295,37 +297,18 @@
         sums_ref[at, columns] = sums_ref[at, columns] + handed[slot : slot + 1, :]
 
 
-def hold_kernel(
-    pieces, here, own, near, far, own_ref, near_ref, far_ref, decays, gains, *rest
-):
-    ends, sums = rest[:pieces], rest[pieces : 2 * pieces]
-    pulled_ref, terms = rest[2 * pieces :]
-    steps, width = pulled_ref.shape
+def hold_local_kernel(
+    own, near, far, own_ref, near_ref, far_ref, decays, gains, terms, slope_ref
+):
+    steps = terms.shape[1]
+    width = terms.shape[0] * LANES
     tiles = steps // SUB
     capacity = own_ref.shape[0]
-    windows = 2 ** (pieces - 1)
-    me = here[0]
-    per = sums[0].shape[0]
-
-    def one(hop, state):
-        window = windows - 1 - hop
-        arriving = jnp.zeros((1, width), jnp.float32)
-        for ahead in range(BACK + 1):
-            reader = jnp.minimum(window + ahead, windows - 1)
-            arriving = arriving + jnp.where(
-                window + ahead < windows, piece_row(sums, per, reader ^ me, BACK - ahead), 0.0
-            )
-        passed = piece_row(ends, 2, window ^ me, 0) * state + arriving
-        return jnp.where(window > me, passed, state)
-
-    incoming = lax.fori_loop(
-        0, windows - 1, one, jnp.zeros((1, width), jnp.float32), unroll=windows <= 8
-    )
     terms[...] = jnp.zeros_like(terms)
     for reader, (place, rows) in enumerate(((own, own_ref), (near, near_ref), (far, far_ref))):
         for slot in range(capacity):
             which, step, first = tile_at(place, slot, steps)
-            mine = (which == BACK - reader) & (place[3 * capacity + slot] == 1)
+            mine = (which == BACK - reader) & (slot < place[3 * capacity])
             step = pl.ds(step, 1)
             for k in range(FB // LANES):
                 terms[first + k, step, :] = terms[first + k, step, :] + jnp.where(
@@ -343,15 +326,52 @@
             factors.append(factor)
         first = decays[k, strided(0, steps), :]
         state, factor = first * state, first * factor
-        carry = incoming[:, lanes(k)]
-        entering = []
+        carry, passed = jnp.zeros((1, LANES), jnp.float32), jnp.ones((1, LANES), jnp.float32)
+        entering, passing = [], []
         for b in range(tiles - 1, -1, -1):
             entering.insert(0, carry)
+            passing.insert(0, passed)
+            passed = factor[b : b + 1, :] * passed
             carry = state[b : b + 1, :] + factor[b : b + 1, :] * carry
         entering = jnp.concatenate(entering, axis=0)
+        passing = jnp.concatenate(passing, axis=0)
         for s in range(SUB):
-            terms[k, strided(SUB - 1 - s, steps), :] = states[s] + factors[s] * entering
-        pulled_ref[:, lanes(k)] = (gains[k] * terms[k]).astype(jnp.bfloat16)
+            at = strided(SUB - 1 - s, steps)
+            gain = gains[k, at, :]
+            terms[k, at, :] = gain * (states[s] + factors[s] * entering)
+            slope_ref[k, at, :] = gain * (factors[s] * passing)
+
+
+def hold_kernel(pieces, here, base_ref, slope_ref, *rest):
+    ends, sums = rest[:pieces], rest[pieces : 2 * pieces]
+    pulled_ref, states, arrivals = rest[2 * pieces :]
+    width = pulled_ref.shape[1]
+    windows = 2 ** (pieces - 1)
+    me = here[0]
+    per = sums[0].shape[0]
+    lay_out(states, ends)
+    lay_out(arrivals, sums)
+
+    def one(hop, state):
+        window = windows - 1 - hop
+        arriving = jnp.zeros((1, width), jnp.float32)
+        for ahead in range(BACK + 1):
+            reader = jnp.minimum(window + ahead, windows - 1)
+            arriving = arriving + jnp.where(
+                window + ahead < windows,
+                arrivals[pl.ds((reader ^ me) * per + BACK - ahead, 1), :],
+                0.0,
+            )
+        passed = states[pl.ds(2 * (window ^ me), 1), :] * state + arriving
+        return jnp.where(window > me, passed, state)
+
+    incoming = lax.fori_loop(
+        0, windows - 1, one, jnp.zeros((1, width), jnp.float32), unroll=windows <= 8
+    )
+    for k in range(width // LANES):
+        pulled_ref[:, lanes(k)] = (base_ref[k] + slope_ref[k] * incoming[:, lanes(k)]).astype(
+            jnp.bfloat16
+        )
 
 
 def image_kernel(
@@ -415,10 +435,10 @@
     f32 = jnp.float32
     columns = pltpu.VMEM((width // LANES, steps, LANES), f32)
     regions = spatial.shape[1] // width
-    devices = lax.axis_size("tm") * lax.axis_size("region")
-
-    live = (jnp.arange(capacity, dtype=jnp.int32)[None] < tile_count).astype(jnp.int32)
-    place = jnp.concatenate([tile_time[0], tile_cell[0], tile_block[0], live], axis=1)[0]
+    windows = lax.axis_size("tm")
+    devices = windows * lax.axis_size("region")
+
+    place = jnp.concatenate([tile_time[0], tile_cell[0], tile_block[0], tile_count], axis=1)[0]
     half = direction.astype(jnp.bfloat16)
     blocks = region_blocks(half)
     part, prefix, decays, gains, last, kept = on_chip(
@@ -439,8 +459,9 @@
         [blocks[3], kept, part, decays, gains, last],
         [(columns.shape, f32), ((2, width), f32)],
     )
+    rows = ((2 * capacity, cells), f32)
     own_rows, near_rows, far_rows = on_chip(
-        gather_kernel, places, [local, prefix], [((2 * capacity, cells), f32)] * (BACK + 1)
+        gather_kernel, places, [local, prefix], [rows] * (BACK + 1)
     )
     near_rows = shifted(near_rows, "tm", 1)
     far_rows = shifted(far_rows, "tm", 2)
@@ -450,7 +471,11 @@
         [here, place],
         [own_rows, near_rows, far_rows, footprint] + ends,
         [((block_count, soundings), f32), ((capacity, cells), f32)],
-        [pltpu.VMEM((SUB, width), f32), pltpu.VMEM((capacity, cells), f32)],
+        [
+            pltpu.VMEM((SUB, width), f32),
+            pltpu.VMEM((capacity, cells), f32),
+            pltpu.VMEM((2 * windows, width), f32),
+        ],
     )
     bit = 1
     while bit < lax.axis_size("region") // 2:
@@ -465,12 +490,21 @@
     )
     near_rows = shifted(rows, "tm", -1)
     far_rows = shifted(rows, "tm", -2)
+    base, slope = on_chip(
+        hold_local_kernel,
+        places,
+        [rows, near_rows, far_rows, decays, gains],
+        [(columns.shape, f32)] * 2,
+    )
     (pulled,) = on_chip(
         lambda *refs: hold_kernel(len(ends), *refs),
-        [here] + places,
-        [rows, near_rows, far_rows, decays, gains] + ends + window_rows(sums),
+        [here],
+        [base, slope] + ends + window_rows(sums),
         [((steps, width), jnp.bfloat16)],
-        [columns],
+        [
+            pltpu.VMEM((2 * windows, width), f32),
+            pltpu.VMEM(((BACK + 2) * windows, width), f32),
+        ],
     )
     blocks = region_blocks(pulled)
     part, kept = on_chip(

time: 94.2 us -> 93.5 us (level)
    pallas_call x11 -> x12, Pallas kernels: 17.5 us -> 17.5 us  [on_chip(): call(*scalars, *arrays, *(pltpu.with_memory_space_constraint(a, pltpu.HBM...]
  transfers between devices with their start and end apart: 20 -> 20, of which waited for: 12 -> 12; matrix products, arithmetic and copies ran while one was open for 0% -> 0% of each run, Pallas kernels for 11% -> 13%
where the time goes in v2:
time: 93.5 us; the launch traced here: 93.2 us
  waiting for transfers between devices  33.5 us (36%)
  starting transfers between devices  28 us (30%)
  Pallas kernels  17.5 us (19%)
  blocking collectives  11.3 us (12%)
  between operations  1.55 us (2%)
  other arithmetic  1.21 us (1%)
    ppermute x14, waiting for transfers between devices, swapped(): lax.ppermute(block, axis, [(i, i ^ bit) for i in range(lax.axis_size(axis...  22.9 us
    pallas_call x12, Pallas kernels, on_chip(): call(*scalars, *arrays, *(pltpu.with_memory_space_constraint(a, pltpu.HBM...  17.5 us
    ppermute x14, starting transfers between devices, swapped(): lax.ppermute(block, axis, [(i, i ^ bit) for i in range(lax.axis_size(axis...  16.8 us
    all_to_all x1, blocking collectives, body(): totals = lax.all_to_all(totals, ('tm', 'region'), 0, 0, tiled=True)  11.3 us
    ppermute x6, starting transfers between devices, shifted(): return lax.ppermute(block, axis, route)  11.2 us
    ppermute x6, waiting for transfers between devices, shifted(): return lax.ppermute(block, axis, route)  10.7 us
  transfers between devices with their start and end apart: 20, of which 12 were waited for; matrix products, arithmetic and copies ran while one was open for 0% of the time, Pallas kernels for 13%

profile of v2, /device:TPU:0, one launch (start us, length us, event | category | flops | bytes accessed | tf_op | source)
XLA Modules:
  0.0 93.2 jit_solution(1182623477891715384)
XLA Ops:
  0.6 1.1 %convert_element_type.3.a_ref = bf16[128,1024]{1,0:T(8,128)(2,1)S(1)} convert(f32[128,1024]{1,0:T(8,128)} %direction_ref.3) | non-fusion elementwise | flops 131072 | bytes 786432 | tf_op jit(solution)/shard_map/convert_element_type | solution.py:442
  1.7 3.1 %collective-permute-start.2 = (bf16[128,1024]{1,0:T(8,128)(2,1)S(1)}, bf16[128,1024]{1,0:T(8,128)(2,1)S(1)}, u32[]{:S(2)}, u32[]{:S(2)}) collective-permute-start(bf16[128,1024]{1,0:T(8,128)(2,1)S(1)} %convert_element_type.3.a_ref), channel_id=1, source_target_pairs={{0,2},{1,3},{2,0},{3,1},{4,6},{5,7},{6,4},{7,5},{8,10},{9,11},{10,... | collective-permute-start | bytes 786440 | tf_op jit(solution)/shard_map/ppermute | solution.py:18
  4.8 0.0 collective-permute-start.4
  4.8 6.3 %collective-permute-done.2.a_ref = bf16[128,1024]{1,0:T(8,128)(2,1)S(1)} collective-permute-done((bf16[128,1024]{1,0:T(8,128)(2,1)S(1)}, bf16[128,1024]{1,0:T(8,128)(2,1)S(1)}, u32[]{:S(2)}, u32[]{:S(2)}) %collective-permute-start.2) | collective-permute-done | bytes 262176 | tf_op jit(solution)/shard_map/ppermute | solution.py:18
  11.1 0.0 collective-permute-start.3
  11.1 0.0 collective-permute-done.4.b_ref
  11.1 4.6 %shard_map.130 = (f32[128,1024]{1,0:T(8,128)S(1)}, f32[8,128,128]{2,1,0:T(8,128)S(1)}, f32[8,128,128]{2,1,0:T(8,128)S(1)}, f32[8,128,128]{2,1,0:T(8,128)S(1)}, f...) custom-call(s32[1]{0:T(128)} %bitcast.region, bf16[128,1024]{1,0:T(8,128)(2,1)S(1)} %convert_element_type.3.a_ref, ...), custom_call_target="tpu_custom_call" | custom-call | tf_op jit(solution)/shard_map/pallas_call | solution.py:69
  15.7 0.0 copy-start.5
  15.7 0.0 copy-start.6
  15.7 0.0 copy-start.7
  15.7 0.0 copy-start.1
  15.8 0.8 shard_map.131.part_ref
  16.6 0.0 copy-start.4
  16.6 0.0 collective-permute-done.3.b_ref
  16.6 1.1 %shard_map.132 = (f32[8,128,128]{2,1,0:T(8,128)S(1)}, f32[2,1024]{1,0:T(2,128)S(1)}) custom-call(s32[1]{0:T(128)} %bitcast.region, bf16[128,1024]{1,0:T(8,128)(2,1)S(1)} %collective-permute-done.3.b_ref, bf16[1024,4096]{1,0:T(8,128)(2,1)S(1)} %get-tuple-element.24.spatial, f32[128,1024]{1,0:T(8,128)S(1)} %shard_map.131.part_ref, ...), custom_call_target="tpu_custom_call" | custom-call | tf_op jit(solution)/shard_map/pallas_call | solution.py:69
  17.7 1.8 %collective-permute-start.7 = (f32[2,1024]{1,0:T(2,128)S(1)}, f32[2,1024]{1,0:T(2,128)S(1)}, u32[]{:S(2)}, u32[]{:S(2)}) collective-permute-start(f32[2,1024]{1,0:T(2,128)S(1)} %get-tuple-element.34.refs_6_.refs_3_), channel_id=1, source_target_pairs={{0,4},{4,0},{8,12},{12,8},{16,20},{20,16},{24,28},{28,24},{1,5},{5... | collective-permute-start | bytes 24584 | tf_op jit(solution)/shard_map/ppermute | solution.py:18
  20.1 1.3 %collective-permute-done.7.refs_7_.refs_4_ = f32[2,1024]{1,0:T(2,128)S(1)} collective-permute-done((f32[2,1024]{1,0:T(2,128)S(1)}, f32[2,1024]{1,0:T(2,128)S(1)}, u32[]{:S(2)}, u32[]{:S(2)}) %collective-permute-start.7) | collective-permute-done | bytes 8224 | tf_op jit(solution)/shard_map/ppermute | solution.py:18
  21.4 1.9 %collective-permute-start.8 = (f32[4,1024]{1,0:T(4,128)S(1)}, f32[4,1024]{1,0:T(4,128)S(1)}, u32[]{:S(2)}, u32[]{:S(2)}) collective-permute-start(f32[4,1024]{1,0:T(4,128)S(1)} %pad_maximum_fusion.3), channel_id=1, source_target_pairs={{0,8},{4,12},{8,0},{12,4},{16,24},{20,28},{24,16},{28,20},{1,9},{5... | collective-permute-start | bytes 49160 | tf_op jit(solution)/shard_map/ppermute | solution.py:18
  23.3 0.0 copy-done.5
  23.3 0.1 add_bitcast_fusion.refs_0_.refs_1_.own
  23.4 1.3 %collective-permute-start = (s32[25]{0:T(128)S(1)}, s32[25]{0:T(128)S(1)}, u32[]{:S(2)}, u32[]{:S(2)}) collective-permute-start(s32[25]{0:T(128)S(1)} %add_bitcast_fusion.refs_0_.refs_1_.own), channel_id=1, source_target_pairs={{4,0},{8,4},{12,8},{16,12},{20,16},{24,20},{28,24},{5,1},{9,5},{13... | collective-permute-start | bytes 308 | tf_op jit(solution)/shard_map/ppermute | solution.py:24
  24.7 1.3 %collective-permute-start.1 = (s32[25]{0:T(128)S(1)}, s32[25]{0:T(128)S(1)}, u32[]{:S(2)}, u32[]{:S(2)}) collective-permute-start(s32[25]{0:T(128)S(1)} %add_bitcast_fusion.refs_0_.refs_1_.own), channel_id=1, source_target_pairs={{8,0},{12,4},{16,8},{20,12},{24,16},{28,20},{9,1},{13,5},{17,9},{2... | collective-permute-start | bytes 308 | tf_op jit(solution)/shard_map/ppermute | solution.py:24
  26.0 2.9 %collective-permute-done.refs_1_.near = s32[25]{0:T(128)S(1)} collective-permute-done((s32[25]{0:T(128)S(1)}, s32[25]{0:T(128)S(1)}, u32[]{:S(2)}, u32[]{:S(2)}) %collective-permute-start) | collective-permute-done | bytes 132 | tf_op jit(solution)/shard_map/ppermute | solution.py:24
  28.8 2.9 %collective-permute-done.1.refs_2_.far = s32[25]{0:T(128)S(1)} collective-permute-done((s32[25]{0:T(128)S(1)}, s32[25]{0:T(128)S(1)}, u32[]{:S(2)}, u32[]{:S(2)}) %collective-permute-start.1) | collective-permute-done | bytes 132 | tf_op jit(solution)/shard_map/ppermute | solution.py:24
  31.7 0.7 shard_map.133
  32.4 3.0 %collective-permute-start.5 = (f32[16,512]{1,0:T(8,128)S(1)}, f32[16,512]{1,0:T(8,128)S(1)}, u32[]{:S(2)}, u32[]{:S(2)}) collective-permute-start(f32[16,512]{1,0:T(8,128)S(1)} %get-tuple-element.32), channel_id=1, source_target_pairs={{0,4},{4,8},{8,12},{12,16},{16,20},{20,24},{24,28},{1,5},{5,9},{9,... | collective-permute-start | bytes 98312 | tf_op jit(solution)/shard_map/ppermute | solution.py:24
  35.4 3.0 %collective-permute-start.6 = (f32[16,512]{1,0:T(8,128)S(1)}, f32[16,512]{1,0:T(8,128)S(1)}, u32[]{:S(2)}, u32[]{:S(2)}) collective-permute-start(f32[16,512]{1,0:T(8,128)S(1)} %get-tuple-element.33), channel_id=1, source_target_pairs={{0,8},{4,12},{8,16},{12,20},{16,24},{20,28},{1,9},{5,13},{9,17},{1... | collective-permute-start | bytes 98312 | tf_op jit(solution)/shard_map/ppermute | solution.py:24
  38.4 0.0 collective-permute-done.8.refs_8_.refs_5_
  38.5 1.5 %collective-permute-start.9 = (f32[8,1024]{1,0:T(8,128)S(1)}, f32[8,1024]{1,0:T(8,128)S(1)}, u32[]{:S(2)}, u32[]{:S(2)}) collective-permute-start(f32[8,1024]{1,0:T(8,128)S(1)} %pad_maximum_fusion.1), channel_id=1, source_target_pairs={{0,16},{4,20},{8,24},{12,28},{16,0},{20,4},{24,8},{28,12},{1,17},{... | collective-permute-start | bytes 98312 | tf_op jit(solution)/shard_map/ppermute | solution.py:18
  40.0 0.0 collective-permute-done.5.refs_3_
  40.0 0.0 collective-permute-done.6.refs_4_
  40.0 3.3 %collective-permute-done.9.refs_9_.refs_6_ = f32[8,1024]{1,0:T(8,128)S(1)} collective-permute-done((f32[8,1024]{1,0:T(8,128)S(1)}, f32[8,1024]{1,0:T(8,128)S(1)}, u32[]{:S(2)}, u32[]{:S(2)}) %collective-permute-start.9) | collective-permute-done | bytes 32800 | tf_op jit(solution)/shard_map/ppermute | solution.py:18
  43.3 1.1 %shard_map.134 = (f32[8,128]{1,0:T(8,128)S(1)}, f32[8,512]{1,0:T(8,128)S(1)}) custom-call(s32[1]{0:T(128)} %bitcast.1.refs_0_, s32[25]{0:T(128)S(1)} %add_bitcast_fusion.refs_0_.refs_1_.own, f32[16,512]{1,0:T(8,128)S(1)} %get-tuple-element.31.refs_2_, f32[16,512]{1,0:T(8,128)S(1)} %collective-permute-done.5.refs_3_, ...), custom_call_target="tpu_custom_call" | custom-call | tf_op jit(solution)/shard_map/pallas_call | solution.py:69
  44.4 0.0 collective-permute-start.10
  44.4 1.2 %collective-permute-done.10 = f32[8,128]{1,0:T(8,128)S(1)} collective-permute-done((f32[8,128]{1,0:T(8,128)S(1)}, f32[8,128]{1,0:T(8,128)S(1)}, u32[]{:S(2)}, u32[]{:S(2)}) %collective-permute-start.10) | collective-permute-done | bytes 4128 | tf_op jit(solution)/shard_map/ppermute | solution.py:18
  45.6 1.5 %collective-permute-start.11 = (f32[8,128]{1,0:T(8,128)S(1)}, f32[8,128]{1,0:T(8,128)S(1)}, u32[]{:S(2)}, u32[]{:S(2)}) collective-permute-start(f32[8,128]{1,0:T(8,128)S(1)} %add.3.refs_1_), channel_id=1, source_target_pairs={{0,2},{1,3},{2,0},{3,1},{4,6},{5,7},{6,4},{7,5},{8,10},{9,11},{10,... | collective-permute-start | bytes 12296 | tf_op jit(solution)/shard_map/ppermute | solution.py:18
  47.1 2.1 %collective-permute-done.11.refs_2_ = f32[8,128]{1,0:T(8,128)S(1)} collective-permute-done((f32[8,128]{1,0:T(8,128)S(1)}, f32[8,128]{1,0:T(8,128)S(1)}, u32[]{:S(2)}, u32[]{:S(2)}) %collective-permute-start.11) | collective-permute-done | bytes 4128 | tf_op jit(solution)/shard_map/ppermute | solution.py:18
  49.2 0.8 shard_map.135
  50.0 1.9 %collective-permute-start.14 = (f32[4,1024]{1,0:T(4,128)S(1)}, f32[4,1024]{1,0:T(4,128)S(1)}, u32[]{:S(2)}, u32[]{:S(2)}) collective-permute-start(f32[4,1024]{1,0:T(4,128)S(1)} %get-tuple-element.40.refs_7_), channel_id=1, source_target_pairs={{0,4},{4,0},{8,12},{12,8},{16,20},{20,16},{24,28},{28,24},{1,5},{5... | collective-permute-start | bytes 49160 | tf_op jit(solution)/shard_map/ppermute | solution.py:18
  51.9 1.9 %collective-permute-done.14.refs_8_ = f32[4,1024]{1,0:T(4,128)S(1)} collective-permute-done((f32[4,1024]{1,0:T(4,128)S(1)}, f32[4,1024]{1,0:T(4,128)S(1)}, u32[]{:S(2)}, u32[]{:S(2)}) %collective-permute-start.14) | collective-permute-done | bytes 16416 | tf_op jit(solution)/shard_map/ppermute | solution.py:18
  53.9 2.1 %collective-permute-start.15 = (f32[8,1024]{1,0:T(8,128)S(1)}, f32[8,1024]{1,0:T(8,128)S(1)}, u32[]{:S(2)}, u32[]{:S(2)}) collective-permute-start(f32[8,1024]{1,0:T(8,128)S(1)} %pad_maximum_fusion.2), channel_id=1, source_target_pairs={{0,8},{4,12},{8,0},{12,4},{16,24},{20,28},{24,16},{28,20},{1,9},{5... | collective-permute-start | bytes 98312 | tf_op jit(solution)/shard_map/ppermute | solution.py:18
  55.9 1.9 %collective-permute-done.15.refs_9_ = f32[8,1024]{1,0:T(8,128)S(1)} collective-permute-done((f32[8,1024]{1,0:T(8,128)S(1)}, f32[8,1024]{1,0:T(8,128)S(1)}, u32[]{:S(2)}, u32[]{:S(2)}) %collective-permute-start.15) | collective-permute-done | bytes 32800 | tf_op jit(solution)/shard_map/ppermute | solution.py:18
  57.9 1.5 %collective-permute-start.16 = (f32[16,1024]{1,0:T(8,128)S(1)}, f32[16,1024]{1,0:T(8,128)S(1)}, u32[]{:S(2)}, u32[]{:S(2)}) collective-permute-start(f32[16,1024]{1,0:T(8,128)S(1)} %pad_maximum_fusion), channel_id=1, source_target_pairs={{0,16},{4,20},{8,24},{12,28},{16,0},{20,4},{24,8},{28,12},{1,17},{... | collective-permute-start | bytes 196616 | tf_op jit(solution)/shard_map/ppermute | solution.py:18
  59.4 1.3 %collective-permute-start.12 = (f32[8,512]{1,0:T(8,128)S(1)}, f32[8,512]{1,0:T(8,128)S(1)}, u32[]{:S(2)}, u32[]{:S(2)}) collective-permute-start(f32[8,512]{1,0:T(8,128)S(1)} %get-tuple-element.37.own_ref), channel_id=1, source_target_pairs={{4,0},{8,4},{12,8},{16,12},{20,16},{24,20},{28,24},{5,1},{9,5},{13... | collective-permute-start | bytes 49160 | tf_op jit(solution)/shard_map/ppermute | solution.py:24
  60.7 1.3 %collective-permute-start.13 = (f32[8,512]{1,0:T(8,128)S(1)}, f32[8,512]{1,0:T(8,128)S(1)}, u32[]{:S(2)}, u32[]{:S(2)}) collective-permute-start(f32[8,512]{1,0:T(8,128)S(1)} %get-tuple-element.37.own_ref), channel_id=1, source_target_pairs={{8,0},{12,4},{16,8},{20,12},{24,16},{28,20},{9,1},{13,5},{17,9},{2... | collective-permute-start | bytes 49160 | tf_op jit(solution)/shard_map/ppermute | solution.py:24
  62.0 3.0 %collective-permute-done.12.near_ref = f32[8,512]{1,0:T(8,128)S(1)} collective-permute-done((f32[8,512]{1,0:T(8,128)S(1)}, f32[8,512]{1,0:T(8,128)S(1)}, u32[]{:S(2)}, u32[]{:S(2)}) %collective-permute-start.12) | collective-permute-done | bytes 16416 | tf_op jit(solution)/shard_map/ppermute | solution.py:24
  65.0 1.9 %collective-permute-done.13.far_ref = f32[8,512]{1,0:T(8,128)S(1)} collective-permute-done((f32[8,512]{1,0:T(8,128)S(1)}, f32[8,512]{1,0:T(8,128)S(1)}, u32[]{:S(2)}, u32[]{:S(2)}) %collective-permute-start.13) | collective-permute-done | bytes 16416 | tf_op jit(solution)/shard_map/ppermute | solution.py:24
  66.9 1.3 %shard_map.136 = (f32[8,128,128]{2,1,0:T(8,128)S(1)}, f32[8,128,128]{2,1,0:T(8,128)S(1)}) custom-call(s32[25]{0:T(128)S(1)} %add_bitcast_fusion.refs_0_.refs_1_.own, s32[25]{0:T(128)S(1)} %collective-permute-done.refs_1_.near, s32[25]{0:T(128)S(1)} %collective-permute-done.1.refs_2_.far, f32[8,512]{1,0:T(8,128)S(1)} %get-tuple-element.37.own_ref, ...), custom_call_target="tpu_custom_call" | custom-call | tf_op jit(solution)/shard_map/pallas_call | solution.py:69
  68.2 0.0 collective-permute-done.16.refs_10_
  68.2 0.1 shard_map.137.a_ref
  68.3 0.0 copy-start
  68.3 0.0 copy-start.2
  68.4 1.6 %collective-permute-start.17 = (bf16[128,1024]{1,0:T(8,128)(2,1)S(1)}, bf16[128,1024]{1,0:T(8,128)(2,1)S(1)}, u32[]{:S(2)}, u32[]{:S(2)}) collective-permute-start(bf16[128,1024]{1,0:T(8,128)(2,1)S(1)} %shard_map.137.a_ref), channel_id=1, source_target_pairs={{0,2},{1,3},{2,0},{3,1},{4,6},{5,7},{6,4},{7,5},{8,10},{9,11},{10,... | collective-permute-start | bytes 786440 | tf_op jit(solution)/shard_map/ppermute | solution.py:18
  69.9 0.0 collective-permute-start.19
  69.9 4.8 %collective-permute-done.17.a_ref = bf16[128,1024]{1,0:T(8,128)(2,1)S(1)} collective-permute-done((bf16[128,1024]{1,0:T(8,128)(2,1)S(1)}, bf16[128,1024]{1,0:T(8,128)(2,1)S(1)}, u32[]{:S(2)}, u32[]{:S(2)}) %collective-permute-start.17) | collective-permute-done | bytes 262176 | tf_op jit(solution)/shard_map/ppermute | solution.py:18
  74.8 0.0 collective-permute-start.18
  74.8 0.0 collective-permute-done.19.b_ref
  74.8 3.8 %shard_map.138 = (f32[128,1024]{1,0:T(8,128)S(1)}, bf16[1024,4096]{1,0:T(8,128)(2,1)S(1)}) custom-call(s32[1]{0:T(128)} %bitcast.region, bf16[128,1024]{1,0:T(8,128)(2,1)S(1)} %shard_map.137.a_ref, bf16[128,1024]{1,0:T(8,128)(2,1)S(1)} %collective-permute-done.19.b_ref, bf16[1024,4096]{1,0:T(8,128)(2,1)} %spatial_hbm.3), custom_call_target="tpu_custom_call" | custom-call | tf_op jit(solution)/shard_map/pallas_call | solution.py:69
  78.6 0.0 copy-start.3
  78.6 0.8 shard_map.139.part_ref
  79.4 0.0 collective-permute-done.18.b_ref
  79.5 1.0 %shard_map.140 = (f32[128,1024]{1,0:T(8,128)S(1)}, f32[32,1,128]{2,1,0:T(1,128)S(1)}) custom-call(s32[1]{0:T(128)} %bitcast.region, bf16[128,1024]{1,0:T(8,128)(2,1)S(1)} %collective-permute-done.18.b_ref, bf16[1024,4096]{1,0:T(8,128)(2,1)S(1)} %get-tuple-element.41.spatial, f32[128,1024]{1,0:T(8,128)S(1)} %shard_map.139.part_ref, f32[128,1024]{1,0:T(8,128)S(1)} %copy-done, ...), custom_call_target="tpu_custom_call" | custom-call | tf_op jit(solution)/shard_map/pallas_call | solution.py:69
  80.5 11.3 %all_to_all.5.totals_ref = f32[32,1,128]{2,1,0:T(1,128)S(1)} all-to-all(f32[32,1,128]{2,1,0:T(1,128)S(1)} %get-tuple-element.43), channel_id=1, replica_groups=mesh['tm'=8,'region'=4] {'tm','region'}, dimensions={0} | all-to-all | bytes 32768 | tf_op jit(solution)/shard_map/all_to_all | solution.py:525
  91.8 1.4 %shard_map.141 = (f32[128,1024]{1,0:T(8,128)}, f32[128,1024]{1,0:T(8,128)}, f32[128,1024]{1,0:T(8,128)}) custom-call(f32[32,1,128]{2,1,0:T(1,128)S(1)} %all_to_all.5.totals_ref, f32[128,1024]{1,0:T(8,128)S(1)} %copy-done.3, f32[128,1024]{1,0:T(8,128)S(1)} %copy-done.2, f32[128,1024]{1,0:T(8,128)S(1)} %copy-done, f32[128,1024]{1,0:T(8,128)S(1)} %get-tuple-element.44.image_ref), custom_call_target="tpu_custom_call" | custom-call | tf_op jit(solution)/shard_map/pallas_call | solution.py:69
  (12 shorter events, 0.1 us)
Async XLA Ops:
  1.7 9.4 %collective-permute-start.2 = (bf16[128,1024]{1,0:T(8,128)(2,1)S(1)}, bf16[128,1024]{1,0:T(8,128)(2,1)S(1)}, u32[]{:S(2)}, u32[]{:S(2)}) collective-permute-start(bf16[128,1024]{1,0:T(8,128)(2,1)S(1)} %convert_element_type.3.a_ref), channel_id=1, source_target_pairs={{0,2},{1,3},{2,0},{3,1},{4,6},{5,7},{6,4},{7,5},{8,10},{9,11},{10,... | collective-permute-start | bytes 786440 | tf_op jit(solution)/shard_map/ppermute | solution.py:18
  4.8 6.3 %collective-permute-start.4 = (bf16[128,1024]{1,0:T(8,128)(2,1)S(1)}, bf16[128,1024]{1,0:T(8,128)(2,1)S(1)}, u32[]{:S(2)}, u32[]{:S(2)}) collective-permute-start(bf16[128,1024]{1,0:T(8,128)(2,1)S(1)} %convert_element_type.3.a_ref), channel_id=1, source_target_pairs={{0,1},{1,0},{2,3},{3,2},{4,5},{5,4},{6,7},{7,6},{8,9},{9,8},{10,11... | collective-permute-start | bytes 786440 | tf_op jit(solution)/shard_map/ppermute | solution.py:18
  11.1 5.5 %collective-permute-start.3 = (bf16[128,1024]{1,0:T(8,128)(2,1)S(1)}, bf16[128,1024]{1,0:T(8,128)(2,1)S(1)}, u32[]{:S(2)}, u32[]{:S(2)}) collective-permute-start(bf16[128,1024]{1,0:T(8,128)(2,1)S(1)} %collective-permute-done.2.a_ref), channel_id=1, source_target_pairs={{0,1},{1,0},{2,3},{3,2},{4,5},{5,4},{6,7},{7,6},{8,9},{9,8},{10,11... | collective-permute-start | bytes 786440 | tf_op jit(solution)/shard_map/ppermute | solution.py:18
  15.7 7.6 %copy-start.5 = (s32[1,1,8]{2,1,0:T(1,128)S(1)}, s32[1,1,8]{2,1,0:T(1,128)}, u32[]{:S(2)}) copy-start(s32[1,1,8]{2,1,0:T(1,128)} %param.17) | copy-start | bytes 100
  15.7 7.6 %copy-start.6 = (s32[1,1,8]{2,1,0:T(1,128)S(1)}, s32[1,1,8]{2,1,0:T(1,128)}, u32[]{:S(2)}) copy-start(s32[1,1,8]{2,1,0:T(1,128)} %param.19) | copy-start | bytes 100
  15.7 7.6 %copy-start.7 = (s32[1,1,8]{2,1,0:T(1,128)S(1)}, s32[1,1,8]{2,1,0:T(1,128)}, u32[]{:S(2)}) copy-start(s32[1,1,8]{2,1,0:T(1,128)} %param.18) | copy-start | bytes 100
  15.7 27.6 %copy-start.1 = (bf16[1,1,8,128,512]{4,3,2,1,0:T(8,128)(2,1)S(1)}, bf16[1,1,8,128,512]{4,3,2,1,0:T(8,128)(2,1)}, u32[]{:S(2)}) copy-start(bf16[1,1,8,128,512]{4,3,2,1,0:T(8,128)(2,1)} %param.16) | copy-start | bytes 3145732
  16.6 32.6 %copy-start.4 = (f32[8,128]{1,0:T(8,128)S(1)}, f32[8,128]{1,0:T(8,128)}, u32[]{:S(2)}) copy-start(f32[8,128]{1,0:T(8,128)} %refs_3_.1) | copy-start | bytes 12292
  17.7 3.7 %collective-permute-start.7 = (f32[2,1024]{1,0:T(2,128)S(1)}, f32[2,1024]{1,0:T(2,128)S(1)}, u32[]{:S(2)}, u32[]{:S(2)}) collective-permute-start(f32[2,1024]{1,0:T(2,128)S(1)} %get-tuple-element.34.refs_6_.refs_3_), channel_id=1, source_target_pairs={{0,4},{4,0},{8,12},{12,8},{16,20},{20,16},{24,28},{28,24},{1,5},{5... | collective-permute-start | bytes 24584 | tf_op jit(solution)/shard_map/ppermute | solution.py:18
  21.4 17.0 %collective-permute-start.8 = (f32[4,1024]{1,0:T(4,128)S(1)}, f32[4,1024]{1,0:T(4,128)S(1)}, u32[]{:S(2)}, u32[]{:S(2)}) collective-permute-start(f32[4,1024]{1,0:T(4,128)S(1)} %pad_maximum_fusion.3), channel_id=1, source_target_pairs={{0,8},{4,12},{8,0},{12,4},{16,24},{20,28},{24,16},{28,20},{1,9},{5... | collective-permute-start | bytes 49160 | tf_op jit(solution)/shard_map/ppermute | solution.py:18
  23.4 5.5 %collective-permute-start = (s32[25]{0:T(128)S(1)}, s32[25]{0:T(128)S(1)}, u32[]{:S(2)}, u32[]{:S(2)}) collective-permute-start(s32[25]{0:T(128)S(1)} %add_bitcast_fusion.refs_0_.refs_1_.own), channel_id=1, source_target_pairs={{4,0},{8,4},{12,8},{16,12},{20,16},{24,20},{28,24},{5,1},{9,5},{13... | collective-permute-start | bytes 308 | tf_op jit(solution)/shard_map/ppermute | solution.py:24
  24.7 7.0 %collective-permute-start.1 = (s32[25]{0:T(128)S(1)}, s32[25]{0:T(128)S(1)}, u32[]{:S(2)}, u32[]{:S(2)}) collective-permute-start(s32[25]{0:T(128)S(1)} %add_bitcast_fusion.refs_0_.refs_1_.own), channel_id=1, source_target_pairs={{8,0},{12,4},{16,8},{20,12},{24,16},{28,20},{9,1},{13,5},{17,9},{2... | collective-permute-start | bytes 308 | tf_op jit(solution)/shard_map/ppermute | solution.py:24
  32.4 7.6 %collective-permute-start.5 = (f32[16,512]{1,0:T(8,128)S(1)}, f32[16,512]{1,0:T(8,128)S(1)}, u32[]{:S(2)}, u32[]{:S(2)}) collective-permute-start(f32[16,512]{1,0:T(8,128)S(1)} %get-tuple-element.32), channel_id=1, source_target_pairs={{0,4},{4,8},{8,12},{12,16},{16,20},{20,24},{24,28},{1,5},{5,9},{9,... | collective-permute-start | bytes 98312 | tf_op jit(solution)/shard_map/ppermute | solution.py:24
  35.4 4.6 %collective-permute-start.6 = (f32[16,512]{1,0:T(8,128)S(1)}, f32[16,512]{1,0:T(8,128)S(1)}, u32[]{:S(2)}, u32[]{:S(2)}) collective-permute-start(f32[16,512]{1,0:T(8,128)S(1)} %get-tuple-element.33), channel_id=1, source_target_pairs={{0,8},{4,12},{8,16},{12,20},{16,24},{20,28},{1,9},{5,13},{9,17},{1... | collective-permute-start | bytes 98312 | tf_op jit(solution)/shard_map/ppermute | solution.py:24
  38.5 4.9 %collective-permute-start.9 = (f32[8,1024]{1,0:T(8,128)S(1)}, f32[8,1024]{1,0:T(8,128)S(1)}, u32[]{:S(2)}, u32[]{:S(2)}) collective-permute-start(f32[8,1024]{1,0:T(8,128)S(1)} %pad_maximum_fusion.1), channel_id=1, source_target_pairs={{0,16},{4,20},{8,24},{12,28},{16,0},{20,4},{24,8},{28,12},{1,17},{... | collective-permute-start | bytes 98312 | tf_op jit(solution)/shard_map/ppermute | solution.py:18
  44.4 1.2 %collective-permute-start.10 = (f32[8,128]{1,0:T(8,128)S(1)}, f32[8,128]{1,0:T(8,128)S(1)}, u32[]{:S(2)}, u32[]{:S(2)}) collective-permute-start(f32[8,128]{1,0:T(8,128)S(1)} %get-tuple-element.35), channel_id=1, source_target_pairs={{0,1},{1,0},{2,3},{3,2},{4,5},{5,4},{6,7},{7,6},{8,9},{9,8},{10,11... | collective-permute-start | bytes 12296 | tf_op jit(solution)/shard_map/ppermute | solution.py:18
  45.6 3.6 %collective-permute-start.11 = (f32[8,128]{1,0:T(8,128)S(1)}, f32[8,128]{1,0:T(8,128)S(1)}, u32[]{:S(2)}, u32[]{:S(2)}) collective-permute-start(f32[8,128]{1,0:T(8,128)S(1)} %add.3.refs_1_), channel_id=1, source_target_pairs={{0,2},{1,3},{2,0},{3,1},{4,6},{5,7},{6,4},{7,5},{8,10},{9,11},{10,... | collective-permute-start | bytes 12296 | tf_op jit(solution)/shard_map/ppermute | solution.py:18
  50.0 3.8 %collective-permute-start.14 = (f32[4,1024]{1,0:T(4,128)S(1)}, f32[4,1024]{1,0:T(4,128)S(1)}, u32[]{:S(2)}, u32[]{:S(2)}) collective-permute-start(f32[4,1024]{1,0:T(4,128)S(1)} %get-tuple-element.40.refs_7_), channel_id=1, source_target_pairs={{0,4},{4,0},{8,12},{12,8},{16,20},{20,16},{24,28},{28,24},{1,5},{5... | collective-permute-start | bytes 49160 | tf_op jit(solution)/shard_map/ppermute | solution.py:18
  53.9 4.0 %collective-permute-start.15 = (f32[8,1024]{1,0:T(8,128)S(1)}, f32[8,1024]{1,0:T(8,128)S(1)}, u32[]{:S(2)}, u32[]{:S(2)}) collective-permute-start(f32[8,1024]{1,0:T(8,128)S(1)} %pad_maximum_fusion.2), channel_id=1, source_target_pairs={{0,8},{4,12},{8,0},{12,4},{16,24},{20,28},{24,16},{28,20},{1,9},{5... | collective-permute-start | bytes 98312 | tf_op jit(solution)/shard_map/ppermute | solution.py:18
  57.9 10.3 %collective-permute-start.16 = (f32[16,1024]{1,0:T(8,128)S(1)}, f32[16,1024]{1,0:T(8,128)S(1)}, u32[]{:S(2)}, u32[]{:S(2)}) collective-permute-start(f32[16,1024]{1,0:T(8,128)S(1)} %pad_maximum_fusion), channel_id=1, source_target_pairs={{0,16},{4,20},{8,24},{12,28},{16,0},{20,4},{24,8},{28,12},{1,17},{... | collective-permute-start | bytes 196616 | tf_op jit(solution)/shard_map/ppermute | solution.py:18
  59.4 5.6 %collective-permute-start.12 = (f32[8,512]{1,0:T(8,128)S(1)}, f32[8,512]{1,0:T(8,128)S(1)}, u32[]{:S(2)}, u32[]{:S(2)}) collective-permute-start(f32[8,512]{1,0:T(8,128)S(1)} %get-tuple-element.37.own_ref), channel_id=1, source_target_pairs={{4,0},{8,4},{12,8},{16,12},{20,16},{24,20},{28,24},{5,1},{9,5},{13... | collective-permute-start | bytes 49160 | tf_op jit(solution)/shard_map/ppermute | solution.py:24
  60.7 6.2 %collective-permute-start.13 = (f32[8,512]{1,0:T(8,128)S(1)}, f32[8,512]{1,0:T(8,128)S(1)}, u32[]{:S(2)}, u32[]{:S(2)}) collective-permute-start(f32[8,512]{1,0:T(8,128)S(1)} %get-tuple-element.37.own_ref), channel_id=1, source_target_pairs={{8,0},{12,4},{16,8},{20,12},{24,16},{28,20},{9,1},{13,5},{17,9},{2... | collective-permute-start | bytes 49160 | tf_op jit(solution)/shard_map/ppermute | solution.py:24
  68.3 11.1 %copy-start = (f32[128,1024]{1,0:T(8,128)S(1)}, f32[128,1024]{1,0:T(8,128)}, u32[]{:S(2)}) copy-start(f32[128,1024]{1,0:T(8,128)} %direction_ref.3) | copy-start | bytes 1572868
  68.3 11.1 %copy-start.2 = (f32[128,1024]{1,0:T(8,128)S(1)}, f32[128,1024]{1,0:T(8,128)}, u32[]{:S(2)}) copy-start(f32[128,1024]{1,0:T(8,128)} %residual_ref.3) | copy-start | bytes 1572868
  68.4 6.4 %collective-permute-start.17 = (bf16[128,1024]{1,0:T(8,128)(2,1)S(1)}, bf16[128,1024]{1,0:T(8,128)(2,1)S(1)}, u32[]{:S(2)}, u32[]{:S(2)}) collective-permute-start(bf16[128,1024]{1,0:T(8,128)(2,1)S(1)} %shard_map.137.a_ref), channel_id=1, source_target_pairs={{0,2},{1,3},{2,0},{3,1},{4,6},{5,7},{6,4},{7,5},{8,10},{9,11},{10,... | collective-permute-start | bytes 786440 | tf_op jit(solution)/shard_map/ppermute | solution.py:18
  69.9 4.9 %collective-permute-start.19 = (bf16[128,1024]{1,0:T(8,128)(2,1)S(1)}, bf16[128,1024]{1,0:T(8,128)(2,1)S(1)}, u32[]{:S(2)}, u32[]{:S(2)}) collective-permute-start(bf16[128,1024]{1,0:T(8,128)(2,1)S(1)} %shard_map.137.a_ref), channel_id=1, source_target_pairs={{0,1},{1,0},{2,3},{3,2},{4,5},{5,4},{6,7},{7,6},{8,9},{9,8},{10,11... | collective-permute-start | bytes 786440 | tf_op jit(solution)/shard_map/ppermute | solution.py:18
  74.8 4.7 %collective-permute-start.18 = (bf16[128,1024]{1,0:T(8,128)(2,1)S(1)}, bf16[128,1024]{1,0:T(8,128)(2,1)S(1)}, u32[]{:S(2)}, u32[]{:S(2)}) collective-permute-start(bf16[128,1024]{1,0:T(8,128)(2,1)S(1)} %collective-permute-done.17.a_ref), channel_id=1, source_target_pairs={{0,1},{1,0},{2,3},{3,2},{4,5},{5,4},{6,7},{7,6},{8,9},{9,8},{10,11... | collective-permute-start | bytes 786440 | tf_op jit(solution)/shard_map/ppermute | solution.py:18
  78.6 13.3 %copy-start.3 = (f32[128,1024]{1,0:T(8,128)S(1)}, f32[128,1024]{1,0:T(8,128)}, u32[]{:S(2)}) copy-start(f32[128,1024]{1,0:T(8,128)} %solution_ref.1) | copy-start | bytes 1572868
